TPU v7x, 32 devices: a whole 2x2x4 slice. The times are simulated.
32 devices in a mesh: grp: 4 (over x, core), mem: 8 (over z, y).
Axes of the slice: x: 2, y: 2, z: 4, core: 2. Of those that a mesh axis runs over, the one named last changes fastest.
Arguments:
- amplitudes: bfloat16 [384, 262144], P('mem', 'grp'), may hold values from -6 to 6
- integrals: bfloat16 [262144, 1024], P(('grp', 'mem')), may hold values from -0.0625 to 0.0625
- irrep_ef: int32 [262144], P(('grp', 'mem')), may hold values from 0 to 7
- irrep_ab: int32 [1024], replicated, may hold values from 0 to 7
Outputs:
- residual: float32 [384, 1024], P('mem', 'grp')
All inputs are finite; a program needn't handle non-finite values.
Results may differ from a plain program's by a relative error of at most 0.0003.
Values may be sent and summed in bfloat16 or wider, within the bound.
No kernel may reach another device: no remote copies, remote signals or barrier semaphores. Data moves between devices by JAX's collectives and lax.ppermute only.
A program may use at most 128 MiB of HBM per device.

v0:
```python
import jax
import jax.numpy as jnp
from jax import lax
from jax.sharding import PartitionSpec as P


def local(amplitudes, integrals, irrep_ef, irrep_ab):
    member_count = lax.axis_size("mem")
    own_rows = amplitudes.shape[0]
    pair_cols = integrals.shape[0]
    allowed = irrep_ef[:, None] == irrep_ab[None, :]
    blocked = jnp.where(allowed, integrals, jnp.zeros_like(integrals))
    shaped = amplitudes.reshape(own_rows, member_count, pair_cols)
    arrived = lax.all_to_all(shaped, "mem", split_axis=1, concat_axis=0, tiled=True)
    partial_value = jnp.dot(
        arrived.reshape(-1, pair_cols), blocked, preferred_element_type=jnp.float32
    )
    row_share = lax.psum_scatter(partial_value, "mem", scatter_dimension=0, tiled=True)
    result = lax.psum_scatter(row_share, "grp", scatter_dimension=1, tiled=True)
    return result


def solution(mesh):
    placed = (P("mem", "grp"), P(("grp", "mem"), None), P(("grp", "mem")), P())
    return jax.shard_map(
        local, mesh=mesh, in_specs=placed, out_specs=P("mem", "grp"), check_vma=False
    )
```

profile of v0, /device:TPU:0, one launch (start us, length us, event | category | flops | bytes accessed | tf_op | source)
XLA Modules:
  0.0 271.0 jit_solution(445686489094129673)
XLA Ops:
  6.5 0.0 reduce-scatter.7.cloned.1.call-start
  6.5 3.2 %copy.15 = bf16[6,8,8,8192]{3,2,0,1:T(8,128)(2,1)S(1)} copy(bf16[6,8,8,8192]{3,2,1,0:T(8,128)(2,1)} %bitcast.14) | data formatting | bytes 12582912 | tf_op jit(solution)/shard_map/reshape | solution.py:13
  9.7 0.0 copy-start
  9.7 0.0 copy-start.1
  9.8 145.3 %all_to_all.15 = bf16[48,8,8192]{2,0,1:T(8,128)(2,1)} all-to-all(bf16[48,8,8192]{2,0,1:T(8,128)(2,1)S(1)} %bitcast.13), channel_id=1, replica_groups=mesh['grp'=4,'mem'=8] {'mem'}, dimensions={1} | all-to-all | bytes 12582912 | tf_op jit(solution)/shard_map/all_to_all | solution.py:14
  155.1 0.0 copy-done
  155.1 0.0 copy-done.1
  155.1 17.7 %fusion.4 = f32[384,1024]{0,1:T(8,128)S(1)} fusion(bf16[384,8192]{1,0:T(8,128)(2,1)} %bitcast.15, bf16[8192,1024]{1,0:T(8,128)(2,1)} %param.5, s32[1024]{0:T(1024)S(1)} %copy-done.1, s32[8192]{0:T(1024)S(1)} %copy-done), kind=kOutput, calls=%fused_computation.6 | convolution fusion | flops 6459228160 | bytes 24678400 | tf_op jit(solution)/shard_map/dot_general | solution.py:15
  172.8 1.6 copy.11
  174.4 0.0 reduce-scatter.7.cloned.1.call-update
  174.5 0.0 reduce-scatter.5.cloned.1.call-start
  174.5 65.1 %reduce-scatter.7.cloned.1.call-done = f32[48,1024]{1,0:T(8,128)} async-done(((f32[384,1024]{1,0:T(8,128)}), f32[48,1024]{1,0:T(8,128)}) %reduce-scatter.7.cloned.1.call-update) | async-done | bytes 196624
  239.6 1.9 copy.12
  241.5 0.0 reduce-scatter.5.cloned.1.call-update
  241.5 21.0 %reduce-scatter.5.cloned.1.call-done = f32[48,256]{0,1:T(8,128)} async-done(((f32[48,1024]{0,1:T(8,128)}), f32[48,256]{0,1:T(8,128)}) %reduce-scatter.5.cloned.1.call-update) | async-done | bytes 49168 | tf_op jit(solution)/shard_map/reduce_scatter | solution.py:19
  262.5 1.6 copy.10
Async XLA Ops:
  6.5 233.0 %reduce-scatter.7.cloned.1.call-start = ((), (), s32[]{:S(2)}) async-start(), calls=%async_computation.4 | async-start | bytes 1769472
  9.7 145.4 %copy-start = (s32[8192]{0:T(1024)S(1)}, s32[8192]{0:T(1024)}, u32[]{:S(2)}) copy-start(s32[8192]{0:T(1024)} %param.6) | copy-start | bytes 98308
  9.7 145.3 %copy-start.1 = (s32[1024]{0:T(1024)S(1)}, s32[1024]{0:T(1024)}, u32[]{:S(2)}) copy-start(s32[1024]{0:T(1024)} %param.7) | copy-start | bytes 12292
  174.5 88.1 %reduce-scatter.5.cloned.1.call-start = ((), (), s32[]{:S(2)}) async-start(), calls=%async_computation.3 | async-start | bytes 655360 | tf_op jit(solution)/shard_map/reduce_scatter | solution.py:19
Sparse Core Ops, SparseCore 0:
  174.6 64.9 reduce-scatter.6
  242.1 20.4 reduce-scatter.4
where the time goes:
time: 271 us
  blocking collectives  145 us (54%)
  waiting for transfers between devices  86.1 us (32%)
  matrix products  17.7 us (7%)
  between operations  13.4 us (5%)
  local copies, waits for them, and re-layouts  8.38 us (3%)
    all_to_all x1, blocking collectives, local(): lax.all_to_all(shaped, 'mem', split_axis=1, concat_axis=0, tiled=True)  145 us
    unnamed x3, waiting for transfers between devices  65.1 us
    reduce_scatter x1, waiting for transfers between devices, local(): result = lax.psum_scatter(row_share, 'grp', scatter_dimension=1, tiled=True)  21 us
    dot_general x1, matrix products, local(): jnp.dot(arrived.reshape(-1, pair_cols), blocked, preferred_element_type=j...  17.7 us
  transfers between devices with their start and end apart: 2, of which 2 were waited for; matrix products, arithmetic and copies ran while one was open for 0% of the time, Pallas kernels for 0%

commit v1 on v0

v1 whole, which is shorter than its diff:
```python
import jax
import jax.numpy as jnp
from jax import lax
from jax.sharding import PartitionSpec as P


def swap(value, axis, distance):
    count = lax.axis_size(axis)
    return lax.ppermute(value, axis, [(i, i ^ distance) for i in range(count)])


def reversed_bits(count):
    levels = count.bit_length() - 1
    return [sum(((p >> i) & 1) << (levels - 1 - i) for i in range(levels)) for p in range(count)]


def issue_order(members):
    half = members // 2
    return [d for j in range(half) for d in (members - 1 - j, half - 1 - j) if d]


def row_chunks(rows):
    if rows % 48:
        return [rows]
    unit = rows // 6
    return [3 * unit, 2 * unit, unit]


def local(amplitudes, integrals, irrep_ef, irrep_ab):
    members = lax.axis_size("mem")
    groups = lax.axis_size("grp")
    me = lax.axis_index("mem")
    group = lax.axis_index("grp")
    pairs = integrals.shape[0]
    width = integrals.shape[1] // groups
    allowed = irrep_ef[:, None] == irrep_ab[None, :]
    blocked = jnp.where(allowed, integrals, jnp.zeros_like(integrals))

    sizes = row_chunks(amplitudes.shape[0])
    starts = [sum(sizes[:i]) for i in range(len(sizes))]
    order = reversed_bits(members)
    arrived = []
    for first, size in zip(starts, sizes):
        got = {}
        for distance in issue_order(members) + [0]:
            column = (me ^ distance) * pairs
            piece = lax.dynamic_slice(amplitudes, (first, column), (size, pairs))
            got[distance] = swap(piece, "mem", distance) if distance else piece
        arrived.append(jnp.concatenate([got[d] for d in order], 0))

    shares = []
    for left in arrived:
        value = jnp.dot(left, blocked, preferred_element_type=jnp.float32)
        tall = value.shape[0]
        blocks = [
            lax.dynamic_slice_in_dim(value, (group ^ j) * width, width, 1)
            for j in range(groups)
        ]
        bit = 1
        while bit < groups:
            sent = jnp.concatenate(blocks[1::2], 0)
            kept = jnp.concatenate(blocks[0::2], 0)
            came = swap(sent, "grp", bit)
            kept = kept + came
            blocks = [kept[i * tall:(i + 1) * tall] for i in range(len(blocks) // 2)]
            bit *= 2
        share = blocks[0]
        bit = 1
        while bit < members:
            half = share.shape[0] // 2
            came = swap(share[half:], "mem", bit)
            share = share[:half] + came
            bit *= 2
        shares.append(share)
    return jnp.concatenate(shares, 0)


def solution(mesh):
    placed = (P("mem", "grp"), P(("grp", "mem"), None), P(("grp", "mem")), P())
    return jax.shard_map(
        local, mesh=mesh, in_specs=placed, out_specs=P("mem", "grp"), check_vma=False
    )
```

time: 271 us -> 226 us (0.83)
  blocking collectives: 145 us -> 0 us
  starting transfers between devices: 0.04 us -> 62.5 us
  waiting for transfers between devices: 86.1 us -> 121 us
  other arithmetic: 0 us -> 16 us
  between operations: 13.4 us -> 0.59 us
  matrix products: 17.7 us -> 14.8 us
    all_to_all x1 -> x0, blocking collectives: 145 us -> none  [local(): lax.all_to_all(shaped, 'mem', split_axis=1, concat_axis=0, tiled=True)]
    ppermute x0 -> x36, waiting for transfers between devices: none -> 121 us  [swap(): return lax.ppermute(value, axis, [(i, i ^ distance) for i in range(count)])]
    unnamed x3 -> x0, waiting for transfers between devices: 65.1 us -> none
    ppermute x0 -> x36, starting transfers between devices: none -> 62.5 us  [swap(): return lax.ppermute(value, axis, [(i, i ^ distance) for i in range(count)])]
    reduce_scatter x1 -> x0, waiting for transfers between devices: 21 us -> none  [local(): result = lax.psum_scatter(row_share, 'grp', scatter_dimension=1, tiled=True)]
    select_n x0 -> x1, other arithmetic: none -> 15.1 us  [local(): blocked = jnp.where(allowed, integrals, jnp.zeros_like(integrals))]
    dynamic_slice x0 -> x6, local copies, waits for them, and re-layouts: none -> 6.08 us  [the longest x3 5.93 us: local(): piece = lax.dynamic_slice(amplitudes, (first, column), (size, pairs))]
    reshape x1 -> x0, local copies, waits for them, and re-layouts: 3.19 us -> none  [local(): shaped = amplitudes.reshape(own_rows, member_count, pair_cols)]
  transfers between devices with their start and end apart: 2 -> 36, of which waited for: 2 -> 23; matrix products, arithmetic and copies ran while one was open for 0% -> 16% of each run, Pallas kernels for 0% -> 0%
where the time goes in v1:
time: 226 us; the launch traced here: 225 us
  waiting for transfers between devices  121 us (54%)
  starting transfers between devices  62.5 us (28%)
  other arithmetic  16 us (7%)
  matrix products  14.8 us (7%)
  local copies, waits for them, and re-layouts  10.5 us (5%)
    ppermute x36, waiting for transfers between devices, swap(): return lax.ppermute(value, axis, [(i, i ^ distance) for i in range(count)])  121 us
    ppermute x36, starting transfers between devices, swap(): return lax.ppermute(value, axis, [(i, i ^ distance) for i in range(count)])  62.5 us
    select_n x1, other arithmetic, local(): blocked = jnp.where(allowed, integrals, jnp.zeros_like(integrals))  15.1 us
    dot_general x3, matrix products, local(): value = jnp.dot(left, blocked, preferred_element_type=jnp.float32)  14.8 us
    dynamic_slice x3, local copies, waits for them, and re-layouts, local(): piece = lax.dynamic_slice(amplitudes, (first, column), (size, pairs))  5.93 us
  transfers between devices with their start and end apart: 36, of which 23 were waited for; matrix products, arithmetic and copies ran while one was open for 16% of the time, Pallas kernels for 0%

profile of v1, /device:TPU:0, one launch (start us, length us, event | category | flops | bytes accessed | tf_op | source)
XLA Modules:
  0.0 225.3 jit_solution(13455006636633831465)
XLA Ops:
  0.0 3.7 %constant_dynamic-slice_fusion.12 = (bf16[24,8192]{1,0:T(8,128)(2,1)}, bf16[24,8192]{1,0:T(8,128)(2,1)}, bf16[24,8192]{1,0:T(8,128)(2,1)}, bf16[24,8192]{1,0:T(8...) fusion(bf16[48,65536]{1,0:T(8,128)(2,1)} %param.4, ...), kind=kLoop, calls=%fused_computation.56 | loop fusion | bytes 6291488 | tf_op jit(solution)/shard_map/dynamic_slice | solution.py:47
  3.7 4.1 %collective-permute-start = (bf16[24,8192]{1,0:T(8,128)(2,1)}, bf16[24,8192]{1,0:T(8,128)(2,1)}, u32[]{:S(2)}, u32[]{:S(2)}) collective-permute-start(bf16[24,8192]{1,0:T(8,128)(2,1)} %get-tuple-element.11), channel_id=1, source_target_pairs={{0,4},{1,5},{2,6},{3,7},{4,0},{5,1},{6,2},{7,3},{8,12},{9,13},{10,... | collective-permute-start | bytes 1179656 | tf_op jit(solution)/shard_map/ppermute | solution.py:9
  7.7 1.6 collective-permute-start.1
  9.3 1.3 constant_dynamic-slice_fusion.26
  10.6 1.9 collective-permute-start.12
  14.5 15.1 %compare_select_fusion = bf16[8192,1024]{1,0:T(8,128)(2,1)} fusion(bf16[8192,1024]{1,0:T(8,128)(2,1)} %param.5, s32[1024]{0:T(1024)S(1)} %copy-done.12, s32[8192]{0:T(1024)S(1)} %copy-done.11), kind=kLoop, calls=%fused_computation | loop fusion | flops 16777216 | bytes 33591296 | tf_op jit(solution)/shard_map/jit(_where)/select_n | solution.py:37
  29.6 29.7 %collective-permute-done.24 = bf16[8,8192]{1,0:T(8,128)(2,1)} collective-permute-done((bf16[8,8192]{1,0:T(8,128)(2,1)}, bf16[8,8192]{1,0:T(8,128)(2,1)}, u32[]{:S(2)}, u32[]{:S(2)}) %collective-permute-start.24) | collective-permute-done | bytes 131104 | tf_op jit(solution)/shard_map/ppermute | solution.py:9
  60.9 3.6 %collective-permute-done.25 = bf16[8,8192]{1,0:T(8,128)(2,1)S(1)} collective-permute-done((bf16[8,8192]{1,0:T(8,128)(2,1)}, bf16[8,8192]{1,0:T(8,128)(2,1)S(1)}, u32[]{:S(2)}, u32[]{:S(2)}) %collective-permute-start.25) | collective-permute-done | bytes 131104 | tf_op jit(solution)/shard_map/ppermute | solution.py:9
  64.5 3.9 %collective-permute-start.26 = (bf16[8,8192]{1,0:T(8,128)(2,1)}, bf16[8,8192]{1,0:T(8,128)(2,1)S(1)}, u32[]{:S(2)}, u32[]{:S(2)}) collective-permute-start(bf16[8,8192]{1,0:T(8,128)(2,1)} %get-tuple-element.24), channel_id=1, source_target_pairs={{0,6},{1,7},{2,4},{3,5},{4,2},{5,3},{6,0},{7,1},{8,14},{9,15},{10,... | collective-permute-start | bytes 393224 | tf_op jit(solution)/shard_map/ppermute | solution.py:9
  68.5 3.1 %collective-permute-done.26 = bf16[8,8192]{1,0:T(8,128)(2,1)S(1)} collective-permute-done((bf16[8,8192]{1,0:T(8,128)(2,1)}, bf16[8,8192]{1,0:T(8,128)(2,1)S(1)}, u32[]{:S(2)}, u32[]{:S(2)}) %collective-permute-start.26) | collective-permute-done | bytes 131104 | tf_op jit(solution)/shard_map/ppermute | solution.py:9
  71.6 1.5 collective-permute-start.27
  73.2 3.6 %collective-permute-done.27 = bf16[8,8192]{1,0:T(8,128)(2,1)S(1)} collective-permute-done((bf16[8,8192]{1,0:T(8,128)(2,1)}, bf16[8,8192]{1,0:T(8,128)(2,1)S(1)}, u32[]{:S(2)}, u32[]{:S(2)}) %collective-permute-start.27) | collective-permute-done | bytes 131104 | tf_op jit(solution)/shard_map/ppermute | solution.py:9
  76.8 4.6 %collective-permute-start.28 = (bf16[8,8192]{1,0:T(8,128)(2,1)}, bf16[8,8192]{1,0:T(8,128)(2,1)S(1)}, u32[]{:S(2)}, u32[]{:S(2)}) collective-permute-start(bf16[8,8192]{1,0:T(8,128)(2,1)} %get-tuple-element.22), channel_id=1, source_target_pairs={{0,5},{1,4},{2,7},{3,6},{4,1},{5,0},{6,3},{7,2},{8,13},{9,12},{10,... | collective-permute-start | bytes 393224 | tf_op jit(solution)/shard_map/ppermute | solution.py:9
  81.4 4.6 %collective-permute-done.28 = bf16[8,8192]{1,0:T(8,128)(2,1)S(1)} collective-permute-done((bf16[8,8192]{1,0:T(8,128)(2,1)}, bf16[8,8192]{1,0:T(8,128)(2,1)S(1)}, u32[]{:S(2)}, u32[]{:S(2)}) %collective-permute-start.28) | collective-permute-done | bytes 131104 | tf_op jit(solution)/shard_map/ppermute | solution.py:9
  86.1 1.4 collective-permute-start.29
  87.5 5.2 %collective-permute-done.29 = bf16[8,8192]{1,0:T(8,128)(2,1)S(1)} collective-permute-done((bf16[8,8192]{1,0:T(8,128)(2,1)}, bf16[8,8192]{1,0:T(8,128)(2,1)S(1)}, u32[]{:S(2)}, u32[]{:S(2)}) %collective-permute-start.29) | collective-permute-done | bytes 131104 | tf_op jit(solution)/shard_map/ppermute | solution.py:9
  92.6 3.5 %collective-permute-start.30 = (bf16[8,8192]{1,0:T(8,128)(2,1)}, bf16[8,8192]{1,0:T(8,128)(2,1)S(1)}, u32[]{:S(2)}, u32[]{:S(2)}) collective-permute-start(bf16[8,8192]{1,0:T(8,128)(2,1)} %get-tuple-element.21), channel_id=1, source_target_pairs={{0,7},{1,6},{2,5},{3,4},{4,3},{5,2},{6,1},{7,0},{8,15},{9,14},{10,... | collective-permute-start | bytes 393224 | tf_op jit(solution)/shard_map/ppermute | solution.py:9
  96.2 5.8 %collective-permute-done.30 = bf16[8,8192]{1,0:T(8,128)(2,1)S(1)} collective-permute-done((bf16[8,8192]{1,0:T(8,128)(2,1)}, bf16[8,8192]{1,0:T(8,128)(2,1)S(1)}, u32[]{:S(2)}, u32[]{:S(2)}) %collective-permute-start.30) | collective-permute-done | bytes 131104 | tf_op jit(solution)/shard_map/ppermute | solution.py:9
  102.0 8.9 %fusion.2 = f32[64,1024]{1,0:T(8,128)S(1)} fusion(bf16[64,8192]{1,0:T(8,128)(2,1)S(1)} %constant_dynamic-update-slice_fusion.14, bf16[8192,1024]{1,0:T(8,128)(2,1)} %compare_select_fusion), kind=kOutput, calls=%fused_computation.79 | convolution fusion | flops 1073741824 | bytes 18087936 | tf_op jit(solution)/shard_map/dot_general | solution.py:53
  111.0 2.5 %collective-permute-start.14 = (bf16[16,8192]{1,0:T(8,128)(2,1)S(1)}, bf16[16,8192]{1,0:T(8,128)(2,1)S(1)}, u32[]{:S(2)}, u32[]{:S(2)}) collective-permute-start(bf16[16,8192]{1,0:T(8,128)(2,1)S(1)} %copy-done.9), channel_id=1, source_target_pairs={{0,6},{1,7},{2,4},{3,5},{4,2},{5,3},{6,0},{7,1},{8,14},{9,15},{10,... | collective-permute-start | bytes 786440 | tf_op jit(solution)/shard_map/ppermute | solution.py:9
  114.5 1.3 collective-permute-start.15
  115.8 6.2 %collective-permute-done.14 = bf16[16,8192]{1,0:T(8,128)(2,1)S(1)} collective-permute-done((bf16[16,8192]{1,0:T(8,128)(2,1)S(1)}, bf16[16,8192]{1,0:T(8,128)(2,1)S(1)}, u32[]{:S(2)}, u32[]{:S(2)}) %collective-permute-start.14) | collective-permute-done | bytes 262176 | tf_op jit(solution)/shard_map/ppermute | solution.py:9
  122.0 5.7 %collective-permute-start.16 = (bf16[16,8192]{1,0:T(8,128)(2,1)S(1)}, bf16[16,8192]{1,0:T(8,128)(2,1)S(1)}, u32[]{:S(2)}, u32[]{:S(2)}) collective-permute-start(bf16[16,8192]{1,0:T(8,128)(2,1)S(1)} %copy-done.7), channel_id=1, source_target_pairs={{0,5},{1,4},{2,7},{3,6},{4,1},{5,0},{6,3},{7,2},{8,13},{9,12},{10,... | collective-permute-start | bytes 786440 | tf_op jit(solution)/shard_map/ppermute | solution.py:9
  127.9 11.2 %collective-permute-done.16 = bf16[16,8192]{1,0:T(8,128)(2,1)S(1)} collective-permute-done((bf16[16,8192]{1,0:T(8,128)(2,1)S(1)}, bf16[16,8192]{1,0:T(8,128)(2,1)S(1)}, u32[]{:S(2)}, u32[]{:S(2)}) %collective-permute-start.16) | collective-permute-done | bytes 262176 | tf_op jit(solution)/shard_map/ppermute | solution.py:9
  139.1 3.1 %collective-permute-start.18 = (bf16[16,8192]{1,0:T(8,128)(2,1)S(1)}, bf16[16,8192]{1,0:T(8,128)(2,1)S(1)}, u32[]{:S(2)}, u32[]{:S(2)}) collective-permute-start(bf16[16,8192]{1,0:T(8,128)(2,1)S(1)} %copy-done.5), channel_id=1, source_target_pairs={{0,7},{1,6},{2,5},{3,4},{4,3},{5,2},{6,1},{7,0},{8,15},{9,14},{10,... | collective-permute-start | bytes 786440 | tf_op jit(solution)/shard_map/ppermute | solution.py:9
  142.4 1.3 collective-permute-done.31
  143.7 1.1 collective-permute-start.3
  144.9 3.5 %collective-permute-done.18 = bf16[16,8192]{1,0:T(8,128)(2,1)S(1)} collective-permute-done((bf16[16,8192]{1,0:T(8,128)(2,1)S(1)}, bf16[16,8192]{1,0:T(8,128)(2,1)S(1)}, u32[]{:S(2)}, u32[]{:S(2)}) %collective-permute-start.18) | collective-permute-done | bytes 262176 | tf_op jit(solution)/shard_map/ppermute | solution.py:9
  148.4 1.5 collective-permute-start.32
  150.0 2.4 %fusion.1 = f32[128,1024]{1,0:T(8,128)S(1)} fusion(bf16[128,8192]{1,0:T(8,128)(2,1)S(1)} %constant_dynamic-update-slice_fusion.7, bf16[8192,1024]{1,0:T(8,128)(2,1)S(1)} %bitcast.7), kind=kOutput, calls=%fused_computation.78 | convolution fusion | flops 2147483648 | bytes 19398656 | tf_op jit(solution)/shard_map/dot_general | solution.py:53
  153.6 3.8 %collective-permute-done.33 = f32[32,256]{1,0:T(8,128)S(1)} collective-permute-done((f32[32,256]{1,0:T(8,128)S(1)}, f32[32,256]{1,0:T(8,128)S(1)}, u32[]{:S(2)}, u32[]{:S(2)}) %collective-permute-start.33) | collective-permute-done | bytes 32800 | tf_op jit(solution)/shard_map/ppermute | solution.py:9
  157.7 3.6 %collective-permute-done.34 = f32[16,256]{1,0:T(8,128)S(1)} collective-permute-done((f32[16,256]{1,0:T(8,128)S(1)}, f32[16,256]{1,0:T(8,128)S(1)}, u32[]{:S(2)}, u32[]{:S(2)}) %collective-permute-start.34) | collective-permute-done | bytes 16416 | tf_op jit(solution)/shard_map/ppermute | solution.py:9
  162.3 2.4 %collective-permute-start.5 = (bf16[24,8192]{1,0:T(8,128)(2,1)S(1)}, bf16[24,8192]{1,0:T(8,128)(2,1)S(1)}, u32[]{:S(2)}, u32[]{:S(2)}) collective-permute-start(bf16[24,8192]{1,0:T(8,128)(2,1)S(1)} %copy-done.2), channel_id=1, source_target_pairs={{0,3},{1,2},{2,1},{3,0},{4,7},{5,6},{6,5},{7,4},{8,11},{9,10},{10,... | collective-permute-start | bytes 1179656 | tf_op jit(solution)/shard_map/ppermute | solution.py:9
  165.8 2.2 collective-permute-start.6
  169.3 13.8 %collective-permute-done.4 = bf16[24,8192]{1,0:T(8,128)(2,1)S(1)} collective-permute-done((bf16[24,8192]{1,0:T(8,128)(2,1)S(1)}, bf16[24,8192]{1,0:T(8,128)(2,1)S(1)}, u32[]{:S(2)}, u32[]{:S(2)}) %collective-permute-start.4) | collective-permute-done | bytes 393248 | tf_op jit(solution)/shard_map/ppermute | solution.py:9
  183.1 6.7 %collective-permute-done.6 = bf16[24,8192]{1,0:T(8,128)(2,1)S(1)} collective-permute-done((bf16[24,8192]{1,0:T(8,128)(2,1)S(1)}, bf16[24,8192]{1,0:T(8,128)(2,1)S(1)}, u32[]{:S(2)}, u32[]{:S(2)}) %collective-permute-start.6) | collective-permute-done | bytes 393248 | tf_op jit(solution)/shard_map/ppermute | solution.py:9
  189.9 3.5 %fusion = f32[192,1024]{1,0:T(8,128)S(1)} fusion(bf16[192,8192]{1,0:T(8,128)(2,1)S(1)} %constant_dynamic-update-slice_fusion, bf16[8192,1024]{1,0:T(8,128)(2,1)S(1)} %bitcast.7), kind=kOutput, calls=%fused_computation.77 | convolution fusion | flops 3221225472 | bytes 20709376 | tf_op jit(solution)/shard_map/dot_general | solution.py:53
  193.6 4.1 %collective-permute-done.35 = f32[8,256]{1,0:T(8,128)S(1)} collective-permute-done((f32[8,256]{1,0:T(8,128)S(1)}, f32[8,256]{1,0:T(8,128)S(1)}, u32[]{:S(2)}, u32[]{:S(2)}) %collective-permute-start.35) | collective-permute-done | bytes 8224 | tf_op jit(solution)/shard_map/ppermute | solution.py:9
  197.7 1.6 collective-permute-start.20
  200.0 4.2 %collective-permute-done.20 = f32[128,256]{1,0:T(8,128)S(1)} collective-permute-done((f32[128,256]{1,0:T(8,128)S(1)}, f32[128,256]{1,0:T(8,128)S(1)}, u32[]{:S(2)}, u32[]{:S(2)}) %collective-permute-start.20) | collective-permute-done | bytes 131104 | tf_op jit(solution)/shard_map/ppermute | solution.py:9
  204.2 1.3 collective-permute-start.21
  205.5 1.7 collective-permute-done.8
  207.2 1.3 collective-permute-start.9
  208.6 5.3 %collective-permute-start.22 = (f32[32,256]{1,0:T(8,128)S(1)}, f32[32,256]{1,0:T(8,128)S(1)}, u32[]{:S(2)}, u32[]{:S(2)}) collective-permute-start(f32[32,256]{1,0:T(8,128)S(1)} %slice.109), channel_id=1, source_target_pairs={{0,2},{1,3},{2,0},{3,1},{4,6},{5,7},{6,4},{7,5},{8,10},{9,11},{10,... | collective-permute-start | bytes 98312 | tf_op jit(solution)/shard_map/ppermute | solution.py:9
  213.8 3.7 %collective-permute-start.10 = (f32[48,256]{1,0:T(8,128)S(1)}, f32[48,256]{1,0:T(8,128)S(1)}, u32[]{:S(2)}, u32[]{:S(2)}) collective-permute-start(f32[48,256]{1,0:T(8,128)S(1)} %slice.101), channel_id=1, source_target_pairs={{0,2},{1,3},{2,0},{3,1},{4,6},{5,7},{6,4},{7,5},{8,10},{9,11},{10,... | collective-permute-start | bytes 147464 | tf_op jit(solution)/shard_map/ppermute | solution.py:9
  218.1 1.7 collective-permute-done.10
  219.9 1.7 collective-permute-start.11
  222.4 2.2 collective-permute-done.11
  (121 shorter events, 13.1 us)
Async XLA Ops:
  3.7 158.7 %collective-permute-start = (bf16[24,8192]{1,0:T(8,128)(2,1)}, bf16[24,8192]{1,0:T(8,128)(2,1)}, u32[]{:S(2)}, u32[]{:S(2)}) collective-permute-start(bf16[24,8192]{1,0:T(8,128)(2,1)} %get-tuple-element.11), channel_id=1, source_target_pairs={{0,4},{1,5},{2,6},{3,7},{4,0},{5,1},{6,2},{7,3},{8,12},{9,13},{10,... | collective-permute-start | bytes 1179656 | tf_op jit(solution)/shard_map/ppermute | solution.py:9
  7.7 158.0 %collective-permute-start.1 = (bf16[24,8192]{1,0:T(8,128)(2,1)}, bf16[24,8192]{1,0:T(8,128)(2,1)}, u32[]{:S(2)}, u32[]{:S(2)}) collective-permute-start(bf16[24,8192]{1,0:T(8,128)(2,1)} %get-tuple-element.10), channel_id=1, source_target_pairs={{0,2},{1,3},{2,0},{3,1},{4,6},{5,7},{6,4},{7,5},{8,10},{9,11},{10,... | collective-permute-start | bytes 1179656 | tf_op jit(solution)/shard_map/ppermute | solution.py:9
  9.3 159.7 %collective-permute-start.2 = (bf16[24,8192]{1,0:T(8,128)(2,1)}, bf16[24,8192]{1,0:T(8,128)(2,1)S(1)}, u32[]{:S(2)}, u32[]{:S(2)}) collective-permute-start(bf16[24,8192]{1,0:T(8,128)(2,1)} %get-tuple-element.9), channel_id=1, source_target_pairs={{0,6},{1,7},{2,4},{3,5},{4,2},{5,3},{6,0},{7,1},{8,14},{9,15},{10,... | collective-permute-start | bytes 1179656 | tf_op jit(solution)/shard_map/ppermute | solution.py:9
  10.6 100.4 %collective-permute-start.12 = (bf16[16,8192]{1,0:T(8,128)(2,1)}, bf16[16,8192]{1,0:T(8,128)(2,1)}, u32[]{:S(2)}, u32[]{:S(2)}) collective-permute-start(bf16[16,8192]{1,0:T(8,128)(2,1)} %get-tuple-element.19), channel_id=1, source_target_pairs={{0,4},{1,5},{2,6},{3,7},{4,0},{5,1},{6,2},{7,3},{8,12},{9,13},{10,... | collective-permute-start | bytes 786440 | tf_op jit(solution)/shard_map/ppermute | solution.py:9
  13.5 45.9 %collective-permute-start.24 = (bf16[8,8192]{1,0:T(8,128)(2,1)}, bf16[8,8192]{1,0:T(8,128)(2,1)}, u32[]{:S(2)}, u32[]{:S(2)}) collective-permute-start(bf16[8,8192]{1,0:T(8,128)(2,1)} %get-tuple-element.26), channel_id=1, source_target_pairs={{0,4},{1,5},{2,6},{3,7},{4,0},{5,1},{6,2},{7,3},{8,12},{9,13},{10,... | collective-permute-start | bytes 393224 | tf_op jit(solution)/shard_map/ppermute | solution.py:9
  59.3 5.2 %collective-permute-start.25 = (bf16[8,8192]{1,0:T(8,128)(2,1)}, bf16[8,8192]{1,0:T(8,128)(2,1)S(1)}, u32[]{:S(2)}, u32[]{:S(2)}) collective-permute-start(bf16[8,8192]{1,0:T(8,128)(2,1)} %get-tuple-element.25), channel_id=1, source_target_pairs={{0,2},{1,3},{2,0},{3,1},{4,6},{5,7},{6,4},{7,5},{8,10},{9,11},{10,... | collective-permute-start | bytes 393224 | tf_op jit(solution)/shard_map/ppermute | solution.py:9
  64.5 7.1 %collective-permute-start.26 = (bf16[8,8192]{1,0:T(8,128)(2,1)}, bf16[8,8192]{1,0:T(8,128)(2,1)S(1)}, u32[]{:S(2)}, u32[]{:S(2)}) collective-permute-start(bf16[8,8192]{1,0:T(8,128)(2,1)} %get-tuple-element.24), channel_id=1, source_target_pairs={{0,6},{1,7},{2,4},{3,5},{4,2},{5,3},{6,0},{7,1},{8,14},{9,15},{10,... | collective-permute-start | bytes 393224 | tf_op jit(solution)/shard_map/ppermute | solution.py:9
  71.6 5.2 %collective-permute-start.27 = (bf16[8,8192]{1,0:T(8,128)(2,1)}, bf16[8,8192]{1,0:T(8,128)(2,1)S(1)}, u32[]{:S(2)}, u32[]{:S(2)}) collective-permute-start(bf16[8,8192]{1,0:T(8,128)(2,1)} %get-tuple-element.23), channel_id=1, source_target_pairs={{0,1},{1,0},{2,3},{3,2},{4,5},{5,4},{6,7},{7,6},{8,9},{9,8},{10,11... | collective-permute-start | bytes 393224 | tf_op jit(solution)/shard_map/ppermute | solution.py:9
  76.8 9.3 %collective-permute-start.28 = (bf16[8,8192]{1,0:T(8,128)(2,1)}, bf16[8,8192]{1,0:T(8,128)(2,1)S(1)}, u32[]{:S(2)}, u32[]{:S(2)}) collective-permute-start(bf16[8,8192]{1,0:T(8,128)(2,1)} %get-tuple-element.22), channel_id=1, source_target_pairs={{0,5},{1,4},{2,7},{3,6},{4,1},{5,0},{6,3},{7,2},{8,13},{9,12},{10,... | collective-permute-start | bytes 393224 | tf_op jit(solution)/shard_map/ppermute | solution.py:9
  86.1 6.6 %collective-permute-start.29 = (bf16[8,8192]{1,0:T(8,128)(2,1)}, bf16[8,8192]{1,0:T(8,128)(2,1)S(1)}, u32[]{:S(2)}, u32[]{:S(2)}) collective-permute-start(bf16[8,8192]{1,0:T(8,128)(2,1)} %get-tuple-element.28), channel_id=1, source_target_pairs={{0,3},{1,2},{2,1},{3,0},{4,7},{5,6},{6,5},{7,4},{8,11},{9,10},{10,... | collective-permute-start | bytes 393224 | tf_op jit(solution)/shard_map/ppermute | solution.py:9
  92.6 9.3 %collective-permute-start.30 = (bf16[8,8192]{1,0:T(8,128)(2,1)}, bf16[8,8192]{1,0:T(8,128)(2,1)S(1)}, u32[]{:S(2)}, u32[]{:S(2)}) collective-permute-start(bf16[8,8192]{1,0:T(8,128)(2,1)} %get-tuple-element.21), channel_id=1, source_target_pairs={{0,7},{1,6},{2,5},{3,4},{4,3},{5,2},{6,1},{7,0},{8,15},{9,14},{10,... | collective-permute-start | bytes 393224 | tf_op jit(solution)/shard_map/ppermute | solution.py:9
  101.9 12.6 %collective-permute-start.13 = (bf16[16,8192]{1,0:T(8,128)(2,1)}, bf16[16,8192]{1,0:T(8,128)(2,1)S(1)}, u32[]{:S(2)}, u32[]{:S(2)}) collective-permute-start(bf16[16,8192]{1,0:T(8,128)(2,1)} %get-tuple-element.18), channel_id=1, source_target_pairs={{0,2},{1,3},{2,0},{3,1},{4,6},{5,7},{6,4},{7,5},{8,10},{9,11},{10,... | collective-permute-start | bytes 786440 | tf_op jit(solution)/shard_map/ppermute | solution.py:9
  101.9 48.0 %slice-start = ((s8[16777216]{0:T(1024)(128)(4,1)}), s8[4194304]{0:T(1024)(128)(4,1)S(1)}, s32[]{:S(2)}) async-start(s8[16777216]{0:T(1024)(128)(4,1)} %bitcast.6), calls=%async_computation | async-start | bytes 8388608
  101.9 12.6 %copy-start.8 = (bf16[16,8192]{1,0:T(8,128)(2,1)S(1)}, bf16[16,8192]{1,0:T(8,128)(2,1)}, u32[]{:S(2)}) copy-start(bf16[16,8192]{1,0:T(8,128)(2,1)} %get-tuple-element.16) | copy-start | bytes 786436
  102.0 20.1 %copy-start.7 = (bf16[16,8192]{1,0:T(8,128)(2,1)S(1)}, bf16[16,8192]{1,0:T(8,128)(2,1)}, u32[]{:S(2)}) copy-start(bf16[16,8192]{1,0:T(8,128)(2,1)} %get-tuple-element.15) | copy-start | bytes 786436
  102.0 25.8 %copy-start.6 = (bf16[16,8192]{1,0:T(8,128)(2,1)S(1)}, bf16[16,8192]{1,0:T(8,128)(2,1)}, u32[]{:S(2)}) copy-start(bf16[16,8192]{1,0:T(8,128)(2,1)} %get-tuple-element.14) | copy-start | bytes 786436
  102.0 37.1 %copy-start.5 = (bf16[16,8192]{1,0:T(8,128)(2,1)S(1)}, bf16[16,8192]{1,0:T(8,128)(2,1)}, u32[]{:S(2)}) copy-start(bf16[16,8192]{1,0:T(8,128)(2,1)} %get-tuple-element.13) | copy-start | bytes 786436
  102.0 47.9 %slice-start.1 = ((s8[16777216]{0:T(1024)(128)(4,1)}), s8[4194304]{0:T(1024)(128)(4,1)S(1)}, s32[]{:S(2)}) async-start(s8[16777216]{0:T(1024)(128)(4,1)} %bitcast.6), calls=%async_computation.1 | async-start | bytes 8388608
  102.0 47.9 %slice-start.2 = ((s8[16777216]{0:T(1024)(128)(4,1)}), s8[4194304]{0:T(1024)(128)(4,1)S(1)}, s32[]{:S(2)}) async-start(s8[16777216]{0:T(1024)(128)(4,1)} %bitcast.6), calls=%async_computation.2 | async-start | bytes 8388608
  102.0 47.9 %slice-start.3 = ((s8[16777216]{0:T(1024)(128)(4,1)}), s8[4194304]{0:T(1024)(128)(4,1)S(1)}, s32[]{:S(2)}) async-start(s8[16777216]{0:T(1024)(128)(4,1)} %bitcast.6), calls=%async_computation.3 | async-start | bytes 8388608
  111.0 32.7 %copy-start.4 = (bf16[24,8192]{1,0:T(8,128)(2,1)S(1)}, bf16[24,8192]{1,0:T(8,128)(2,1)}, u32[]{:S(2)}) copy-start(bf16[24,8192]{1,0:T(8,128)(2,1)} %get-tuple-element.8) | copy-start | bytes 1179652
  111.0 11.0 %collective-permute-start.14 = (bf16[16,8192]{1,0:T(8,128)(2,1)S(1)}, bf16[16,8192]{1,0:T(8,128)(2,1)S(1)}, u32[]{:S(2)}, u32[]{:S(2)}) collective-permute-start(bf16[16,8192]{1,0:T(8,128)(2,1)S(1)} %copy-done.9), channel_id=1, source_target_pairs={{0,6},{1,7},{2,4},{3,5},{4,2},{5,3},{6,0},{7,1},{8,14},{9,15},{10,... | collective-permute-start | bytes 786440 | tf_op jit(solution)/shard_map/ppermute | solution.py:9
  114.5 13.3 %collective-permute-start.15 = (bf16[16,8192]{1,0:T(8,128)(2,1)S(1)}, bf16[16,8192]{1,0:T(8,128)(2,1)S(1)}, u32[]{:S(2)}, u32[]{:S(2)}) collective-permute-start(bf16[16,8192]{1,0:T(8,128)(2,1)S(1)} %copy-done.8), channel_id=1, source_target_pairs={{0,1},{1,0},{2,3},{3,2},{4,5},{5,4},{6,7},{7,6},{8,9},{9,8},{10,11... | collective-permute-start | bytes 786440 | tf_op jit(solution)/shard_map/ppermute | solution.py:9
  122.0 17.1 %collective-permute-start.16 = (bf16[16,8192]{1,0:T(8,128)(2,1)S(1)}, bf16[16,8192]{1,0:T(8,128)(2,1)S(1)}, u32[]{:S(2)}, u32[]{:S(2)}) collective-permute-start(bf16[16,8192]{1,0:T(8,128)(2,1)S(1)} %copy-done.7), channel_id=1, source_target_pairs={{0,5},{1,4},{2,7},{3,6},{4,1},{5,0},{6,3},{7,2},{8,13},{9,12},{10,... | collective-permute-start | bytes 786440 | tf_op jit(solution)/shard_map/ppermute | solution.py:9
  127.8 14.5 %collective-permute-start.17 = (bf16[16,8192]{1,0:T(8,128)(2,1)S(1)}, bf16[16,8192]{1,0:T(8,128)(2,1)S(1)}, u32[]{:S(2)}, u32[]{:S(2)}) collective-permute-start(bf16[16,8192]{1,0:T(8,128)(2,1)S(1)} %copy-done.6), channel_id=1, source_target_pairs={{0,3},{1,2},{2,1},{3,0},{4,7},{5,6},{6,5},{7,4},{8,11},{9,10},{10,... | collective-permute-start | bytes 786440 | tf_op jit(solution)/shard_map/ppermute | solution.py:9
  139.1 9.3 %collective-permute-start.18 = (bf16[16,8192]{1,0:T(8,128)(2,1)S(1)}, bf16[16,8192]{1,0:T(8,128)(2,1)S(1)}, u32[]{:S(2)}, u32[]{:S(2)}) collective-permute-start(bf16[16,8192]{1,0:T(8,128)(2,1)S(1)} %copy-done.5), channel_id=1, source_target_pairs={{0,7},{1,6},{2,5},{3,4},{4,3},{5,2},{6,1},{7,0},{8,15},{9,14},{10,... | collective-permute-start | bytes 786440 | tf_op jit(solution)/shard_map/ppermute | solution.py:9
  142.3 1.4 collective-permute-start.31
  143.7 25.4 %collective-permute-start.3 = (bf16[24,8192]{1,0:T(8,128)(2,1)S(1)}, bf16[24,8192]{1,0:T(8,128)(2,1)S(1)}, u32[]{:S(2)}, u32[]{:S(2)}) collective-permute-start(bf16[24,8192]{1,0:T(8,128)(2,1)S(1)} %copy-done.4), channel_id=1, source_target_pairs={{0,1},{1,0},{2,3},{3,2},{4,5},{5,4},{6,7},{7,6},{8,9},{9,8},{10,11... | collective-permute-start | bytes 1179656 | tf_op jit(solution)/shard_map/ppermute | solution.py:9
  148.4 4.3 %collective-permute-start.32 = (f32[64,256]{1,0:T(8,128)S(1)}, f32[64,256]{1,0:T(8,128)S(1)}, u32[]{:S(2)}, u32[]{:S(2)}) collective-permute-start(f32[64,256]{1,0:T(8,128)S(1)} %slice.113), channel_id=1, source_target_pairs={{0,16},{8,24},{16,0},{24,8},{1,17},{9,25},{17,1},{25,9},{2,18},{10... | collective-permute-start | bytes 196616 | tf_op jit(solution)/shard_map/ppermute | solution.py:9
  149.9 12.4 %copy-start.2 = (bf16[24,8192]{1,0:T(8,128)(2,1)S(1)}, bf16[24,8192]{1,0:T(8,128)(2,1)}, u32[]{:S(2)}) copy-start(bf16[24,8192]{1,0:T(8,128)(2,1)} %get-tuple-element.6) | copy-start | bytes 1179652
  150.0 14.8 %copy-start.10 = (bf16[192,8192]{1,0:T(8,128)(2,1)S(1)}, bf16[192,8192]{1,0:T(8,128)(2,1)}, u32[]{:S(2)}) copy-start(bf16[192,8192]{1,0:T(8,128)(2,1)} %get-tuple-element.12) | copy-start | bytes 9437188
  150.0 15.8 %copy-start.1 = (bf16[24,8192]{1,0:T(8,128)(2,1)S(1)}, bf16[24,8192]{1,0:T(8,128)(2,1)}, u32[]{:S(2)}) copy-start(bf16[24,8192]{1,0:T(8,128)(2,1)} %get-tuple-element.5) | copy-start | bytes 1179652
  152.7 4.7 %collective-permute-start.33 = (f32[32,256]{1,0:T(8,128)S(1)}, f32[32,256]{1,0:T(8,128)S(1)}, u32[]{:S(2)}, u32[]{:S(2)}) collective-permute-start(f32[32,256]{1,0:T(8,128)S(1)} %slice.115), channel_id=1, source_target_pairs={{0,1},{1,0},{2,3},{3,2},{4,5},{5,4},{6,7},{7,6},{8,9},{9,8},{10,11... | collective-permute-start | bytes 98312 | tf_op jit(solution)/shard_map/ppermute | solution.py:9
  157.4 3.8 %collective-permute-start.34 = (f32[16,256]{1,0:T(8,128)S(1)}, f32[16,256]{1,0:T(8,128)S(1)}, u32[]{:S(2)}, u32[]{:S(2)}) collective-permute-start(f32[16,256]{1,0:T(8,128)S(1)} %slice.117), channel_id=1, source_target_pairs={{0,2},{1,3},{2,0},{3,1},{4,6},{5,7},{6,4},{7,5},{8,10},{9,11},{10,... | collective-permute-start | bytes 49160 | tf_op jit(solution)/shard_map/ppermute | solution.py:9
  161.2 21.8 %collective-permute-start.4 = (bf16[24,8192]{1,0:T(8,128)(2,1)S(1)}, bf16[24,8192]{1,0:T(8,128)(2,1)S(1)}, u32[]{:S(2)}, u32[]{:S(2)}) collective-permute-start(bf16[24,8192]{1,0:T(8,128)(2,1)S(1)} %copy-done.3), channel_id=1, source_target_pairs={{0,5},{1,4},{2,7},{3,6},{4,1},{5,0},{6,3},{7,2},{8,13},{9,12},{10,... | collective-permute-start | bytes 1179656 | tf_op jit(solution)/shard_map/ppermute | solution.py:9
  162.3 20.7 %collective-permute-start.5 = (bf16[24,8192]{1,0:T(8,128)(2,1)S(1)}, bf16[24,8192]{1,0:T(8,128)(2,1)S(1)}, u32[]{:S(2)}, u32[]{:S(2)}) collective-permute-start(bf16[24,8192]{1,0:T(8,128)(2,1)S(1)} %copy-done.2), channel_id=1, source_target_pairs={{0,3},{1,2},{2,1},{3,0},{4,7},{5,6},{6,5},{7,4},{8,11},{9,10},{10,... | collective-permute-start | bytes 1179656 | tf_op jit(solution)/shard_map/ppermute | solution.py:9
  165.8 24.1 %collective-permute-start.6 = (bf16[24,8192]{1,0:T(8,128)(2,1)S(1)}, bf16[24,8192]{1,0:T(8,128)(2,1)S(1)}, u32[]{:S(2)}, u32[]{:S(2)}) collective-permute-start(bf16[24,8192]{1,0:T(8,128)(2,1)S(1)} %copy-done.1), channel_id=1, source_target_pairs={{0,7},{1,6},{2,5},{3,4},{4,3},{5,2},{6,1},{7,0},{8,15},{9,14},{10,... | collective-permute-start | bytes 1179656 | tf_op jit(solution)/shard_map/ppermute | solution.py:9
  169.0 28.6 %collective-permute-start.19 = (f32[256,256]{1,0:T(8,128)S(1)}, f32[256,256]{1,0:T(8,128)S(1)}, u32[]{:S(2)}, u32[]{:S(2)}) collective-permute-start(f32[256,256]{1,0:T(8,128)S(1)} %pad_maximum_fusion.1), channel_id=1, source_target_pairs={{0,8},{8,0},{16,24},{24,16},{1,9},{9,1},{17,25},{25,17},{2,10},{10... | collective-permute-start | bytes 786440 | tf_op jit(solution)/shard_map/ppermute | solution.py:9
  169.1 28.5 %collective-permute-start.35 = (f32[8,256]{1,0:T(8,128)S(1)}, f32[8,256]{1,0:T(8,128)S(1)}, u32[]{:S(2)}, u32[]{:S(2)}) collective-permute-start(f32[8,256]{1,0:T(8,128)S(1)} %slice.119), channel_id=1, source_target_pairs={{0,4},{1,5},{2,6},{3,7},{4,0},{5,1},{6,2},{7,3},{8,12},{9,13},{10,... | collective-permute-start | bytes 24584 | tf_op jit(solution)/shard_map/ppermute | solution.py:9
  193.5 5.8 %collective-permute-start.7 = (f32[384,256]{1,0:T(8,128)S(1)}, f32[384,256]{1,0:T(8,128)S(1)}, u32[]{:S(2)}, u32[]{:S(2)}) collective-permute-start(f32[384,256]{1,0:T(8,128)S(1)} %pad_maximum_fusion), channel_id=1, source_target_pairs={{0,8},{8,0},{16,24},{24,16},{1,9},{9,1},{17,25},{25,17},{2,10},{10... | collective-permute-start | bytes 1179656 | tf_op jit(solution)/shard_map/ppermute | solution.py:9
  197.7 6.4 %collective-permute-start.20 = (f32[128,256]{1,0:T(8,128)S(1)}, f32[128,256]{1,0:T(8,128)S(1)}, u32[]{:S(2)}, u32[]{:S(2)}) collective-permute-start(f32[128,256]{1,0:T(8,128)S(1)} %slice.105), channel_id=1, source_target_pairs={{0,16},{8,24},{16,0},{24,8},{1,17},{9,25},{17,1},{25,9},{2,18},{10... | collective-permute-start | bytes 393224 | tf_op jit(solution)/shard_map/ppermute | solution.py:9
  199.4 7.8 %collective-permute-start.8 = (f32[192,256]{1,0:T(8,128)S(1)}, f32[192,256]{1,0:T(8,128)S(1)}, u32[]{:S(2)}, u32[]{:S(2)}) collective-permute-start(f32[192,256]{1,0:T(8,128)S(1)} %slice.97), channel_id=1, source_target_pairs={{0,16},{8,24},{16,0},{24,8},{1,17},{9,25},{17,1},{25,9},{2,18},{10... | collective-permute-start | bytes 589832 | tf_op jit(solution)/shard_map/ppermute | solution.py:9
  204.2 4.3 %collective-permute-start.21 = (f32[64,256]{1,0:T(8,128)S(1)}, f32[64,256]{1,0:T(8,128)S(1)}, u32[]{:S(2)}, u32[]{:S(2)}) collective-permute-start(f32[64,256]{1,0:T(8,128)S(1)} %slice.107), channel_id=1, source_target_pairs={{0,1},{1,0},{2,3},{3,2},{4,5},{5,4},{6,7},{7,6},{8,9},{9,8},{10,11... | collective-permute-start | bytes 196616 | tf_op jit(solution)/shard_map/ppermute | solution.py:9
  207.2 6.6 %collective-permute-start.9 = (f32[96,256]{1,0:T(8,128)S(1)}, f32[96,256]{1,0:T(8,128)S(1)}, u32[]{:S(2)}, u32[]{:S(2)}) collective-permute-start(f32[96,256]{1,0:T(8,128)S(1)} %slice.99), channel_id=1, source_target_pairs={{0,1},{1,0},{2,3},{3,2},{4,5},{5,4},{6,7},{7,6},{8,9},{9,8},{10,11... | collective-permute-start | bytes 294920 | tf_op jit(solution)/shard_map/ppermute | solution.py:9
  208.6 9.0 %collective-permute-start.22 = (f32[32,256]{1,0:T(8,128)S(1)}, f32[32,256]{1,0:T(8,128)S(1)}, u32[]{:S(2)}, u32[]{:S(2)}) collective-permute-start(f32[32,256]{1,0:T(8,128)S(1)} %slice.109), channel_id=1, source_target_pairs={{0,2},{1,3},{2,0},{3,1},{4,6},{5,7},{6,4},{7,5},{8,10},{9,11},{10,... | collective-permute-start | bytes 98312 | tf_op jit(solution)/shard_map/ppermute | solution.py:9
  213.8 6.0 %collective-permute-start.10 = (f32[48,256]{1,0:T(8,128)S(1)}, f32[48,256]{1,0:T(8,128)S(1)}, u32[]{:S(2)}, u32[]{:S(2)}) collective-permute-start(f32[48,256]{1,0:T(8,128)S(1)} %slice.101), channel_id=1, source_target_pairs={{0,2},{1,3},{2,0},{3,1},{4,6},{5,7},{6,4},{7,5},{8,10},{9,11},{10,... | collective-permute-start | bytes 147464 | tf_op jit(solution)/shard_map/ppermute | solution.py:9
  217.6 4.8 %collective-permute-start.23 = (f32[16,256]{1,0:T(8,128)S(1)}, f32[16,256]{1,0:T(8,128)S(1)}, u32[]{:S(2)}, u32[]{:S(2)}) collective-permute-start(f32[16,256]{1,0:T(8,128)S(1)} %slice.111), channel_id=1, source_target_pairs={{0,4},{1,5},{2,6},{3,7},{4,0},{5,1},{6,2},{7,3},{8,12},{9,13},{10,... | collective-permute-start | bytes 49160 | tf_op jit(solution)/shard_map/ppermute | solution.py:9
  219.9 4.8 %collective-permute-start.11 = (f32[24,256]{1,0:T(8,128)S(1)}, f32[24,256]{1,0:T(8,128)S(1)}, u32[]{:S(2)}, u32[]{:S(2)}) collective-permute-start(f32[24,256]{1,0:T(8,128)S(1)} %slice.103), channel_id=1, source_target_pairs={{0,4},{1,5},{2,6},{3,7},{4,0},{5,1},{6,2},{7,3},{8,12},{9,13},{10,... | collective-permute-start | bytes 73736 | tf_op jit(solution)/shard_map/ppermute | solution.py:9
  (5 other events, 40.1 us)

commit v2 on v0

v2 whole, which is shorter than its diff:
```python
import jax
import jax.numpy as jnp
from jax import lax
from jax.experimental import pallas as pl
from jax.experimental.pallas import tpu as pltpu
from jax.sharding import PartitionSpec as P

SHARES = (1, 2, 3)
LANES = 128


def swap(value, axis, distance):
    count = lax.axis_size(axis)
    return lax.ppermute(value, axis, [(i, i ^ distance) for i in range(count)])


def reversed_bits(count):
    levels = count.bit_length() - 1
    return [sum(((p >> i) & 1) << (levels - 1 - i) for i in range(levels)) for p in range(count)]


def row_chunks(rows):
    if rows % (8 * sum(SHARES)):
        return [rows]
    unit = rows // sum(SHARES)
    return [share * unit for share in SHARES]


def blocked_dot_kernel(group, *refs):
    pieces, (values, labels, targets, kept, sent, total) = refs[:-6], refs[-6:]
    left = jnp.concatenate([piece[...] for piece in pieces], 0)
    label = labels[...]
    columns = []
    for j in range(values.shape[1] // LANES):
        at = slice(j * LANES, (j + 1) * LANES)
        part = values[:, at]
        columns.append(jnp.where(label == targets[:, at], part, jnp.zeros_like(part)))
    term = jnp.dot(left, jnp.concatenate(columns, 1), preferred_element_type=jnp.float32)
    step = pl.program_id(0)

    @pl.when(step == 0)
    def _():
        total[...] = term

    @pl.when(step > 0)
    def _():
        total[...] += term

    @pl.when(step == pl.num_programs(0) - 1)
    def _():
        rows, width = total.shape[0], kept.shape[1]
        groups = total.shape[1] // width
        for j in range(groups):
            start = pl.multiple_of((group[0] ^ j) * width, LANES)
            out = sent if j % 2 else kept
            out[(j // 2) * rows:(j // 2 + 1) * rows, :] = total[:, pl.ds(start, width)]


def blocked_dot(pieces, values, labels, targets, group, groups):
    pairs, columns = values.shape
    rows = sum(piece.shape[0] for piece in pieces)
    slab = next(s for s in (2048, 1024, 512, 256, 128, pairs) if pairs % s == 0)
    width = columns // groups
    half = jax.ShapeDtypeStruct((rows * groups // 2, width), jnp.float32)
    spec = pltpu.PrefetchScalarGridSpec(
        num_scalar_prefetch=1,
        grid=(pairs // slab,),
        in_specs=[pl.BlockSpec((piece.shape[0], slab), lambda k, g: (0, k)) for piece in pieces]
        + [
            pl.BlockSpec((slab, columns), lambda k, g: (k, 0)),
            pl.BlockSpec((slab, LANES), lambda k, g: (k, 0)),
            pl.BlockSpec((1, columns), lambda k, g: (0, 0)),
        ],
        out_specs=[pl.BlockSpec(half.shape, lambda k, g: (0, 0))] * 2,
        scratch_shapes=[pltpu.VMEM((rows, columns), jnp.float32)],
    )
    return pl.pallas_call(
        blocked_dot_kernel,
        grid_spec=spec,
        out_shape=[half, half],
        cost_estimate=pl.CostEstimate(
            flops=2 * rows * pairs * columns, bytes_accessed=2 * pairs * columns, transcendentals=0
        ),
        compiler_params=pltpu.CompilerParams(vmem_limit_bytes=16 << 20),
    )(group, *pieces, values, labels, targets)


def columns_to_owner(pieces, blocked, groups):
    kept, sent = blocked(pieces)
    bit = 1
    while bit < groups:
        came = swap(sent, "grp", bit)
        kept = kept + came
        bit *= 2
        if bit < groups:
            tall = kept.shape[0] * bit // groups
            blocks = [kept[i * tall:(i + 1) * tall] for i in range(groups // bit)]
            kept, sent = jnp.concatenate(blocks[0::2], 0), jnp.concatenate(blocks[1::2], 0)
    return kept


def fold(shares, distance):
    halves = [share.shape[0] // 2 for share in shares]
    out = jnp.concatenate([share[h:] for share, h in zip(shares, halves)], 0)
    came = swap(out, "mem", distance)
    kept = jnp.concatenate([share[:h] for share, h in zip(shares, halves)], 0) + came
    return cut(kept, halves)


def cut(value, sizes):
    ends = [sum(sizes[:i]) for i in range(len(sizes) + 1)]
    return [value[i:j] for i, j in zip(ends, ends[1:])]


def local(amplitudes, integrals, irrep_ef, irrep_ab):
    members = lax.axis_size("mem")
    groups = lax.axis_size("grp")
    me = lax.axis_index("mem")
    group = jnp.reshape(lax.axis_index("grp"), (1,)).astype(jnp.int32)
    rows, pairs = amplitudes.shape[0], integrals.shape[0]
    half, quarter = members // 2, members // 4
    labels = jnp.broadcast_to(irrep_ef.astype(jnp.bfloat16)[:, None], (pairs, LANES))
    targets = irrep_ab.astype(jnp.bfloat16)[None, :]

    def blocked(pieces):
        if any(piece.shape[0] % 8 for piece in pieces):
            pieces = [jnp.concatenate(pieces, 0)]
        return blocked_dot(pieces, integrals, labels, targets, group, groups)

    sizes = row_chunks(rows)
    far_ranges = [(sum(sizes[:c]), size) for c, size in enumerate(sizes)]
    near_ranges = [(0, sizes[0])] + [(sizes[0], rows - sizes[0])] * (len(sizes) > 1)
    source = amplitudes

    def piece(span, distance):
        return lax.dynamic_slice(source, (span[0], (me ^ distance) * pairs), (span[1], pairs))

    lead = piece(far_ranges[0], members - 1)
    source, lead = lax.optimization_barrier((source, lead))
    far, near = [], []
    for c, span in enumerate(far_ranges):
        outs = {d: lead if c == 0 and d == members - 1 else piece(span, d) for d in range(half, members)}
        far.append({d: swap(out, "mem", d) for d, out in outs.items()})
    for span in near_ranges:
        outs = {d: piece(span, d) for d in range(half)}
        near.append({d: swap(out, "mem", d) if d else out for d, out in outs.items()})

    order = reversed_bits(half)
    far_shares, near_shares = [], []
    for c, got in enumerate(near):
        parts = [[got[d] for d in order]]
        if c < len(far) - 1:
            parts.append([far[c][half + d] for d in order])
        kept = columns_to_owner(sum(parts, []), blocked, groups)
        shares = cut(kept, [sum(p.shape[0] for p in part) for part in parts])
        if half > 1:
            shares = fold(shares, 1)
        near_shares.append(shares[0])
        far_shares += shares[1:]
    bit = 2
    while bit < half:
        shares = fold(near_shares + far_shares, bit)
        near_shares, far_shares = shares[:len(near_shares)], shares[len(near_shares):]
        bit *= 2
    across = []
    if far_shares:
        across.append(swap(jnp.concatenate(far_shares, 0), "mem", half))
    total = None
    for low in (half + quarter, half):
        ends = [far[-1][low + d] for d in range(quarter)]
        share = columns_to_owner(ends, blocked, groups)
        for d, block in reversed(list(enumerate(cut(share, [sizes[-1]] * quarter)))):
            came = swap(block, "mem", low + d)
            total = came if total is None else total + came
    return jnp.concatenate(near_shares, 0) + jnp.concatenate(across + [total], 0)


def solution(mesh):
    placed = (P("mem", "grp"), P(("grp", "mem"), None), P(("grp", "mem")), P())
    return jax.shard_map(
        local, mesh=mesh, in_specs=placed, out_specs=P("mem", "grp"), check_vma=False
    )
```

time: 271 us -> 174 us (0.64)
  blocking collectives: 145 us -> 0 us
  starting transfers between devices: 0.04 us -> 58.8 us
  Pallas kernels: 0 us -> 18.1 us
  matrix products: 17.7 us -> 0 us
  between operations: 13.4 us -> 0.33 us
  local copies, waits for them, and re-layouts: 8.38 us -> 17.1 us
  waiting for transfers between devices: 86.1 us -> 77.4 us
    all_to_all x1 -> x0, blocking collectives: 145 us -> none  [local(): lax.all_to_all(shaped, 'mem', split_axis=1, concat_axis=0, tiled=True)]
    ppermute x0 -> x34, waiting for transfers between devices: none -> 77.4 us  [swap(): return lax.ppermute(value, axis, [(i, i ^ distance) for i in range(count)])]
    unnamed x3 -> x0, waiting for transfers between devices: 65.1 us -> none
    ppermute x0 -> x34, starting transfers between devices: none -> 58.8 us  [swap(): return lax.ppermute(value, axis, [(i, i ^ distance) for i in range(count)])]
    reduce_scatter x1 -> x0, waiting for transfers between devices: 21 us -> none  [local(): result = lax.psum_scatter(row_share, 'grp', scatter_dimension=1, tiled=True)]
    pallas_call x0 -> x4, Pallas kernels: none -> 18.1 us  [blocked_dot(): pl.pallas_call(blocked_dot_kernel, grid_spec=spec, out_shape=[half, half]...]
    dot_general x1 -> x0, matrix products: 17.7 us -> none  [local(): jnp.dot(arrived.reshape(-1, pair_cols), blocked, preferred_element_type=j...]
    dynamic_slice x0 -> x5, local copies, waits for them, and re-layouts: none -> 7.24 us  [piece(): lax.dynamic_slice(source, (span[0], (me ^ distance) * pairs), (span[1], p...]
  transfers between devices with their start and end apart: 2 -> 34, of which waited for: 2 -> 10; matrix products, arithmetic and copies ran while one was open for 0% -> 7% of each run, Pallas kernels for 0% -> 10%
where the time goes in v2:
time: 174 us
  waiting for transfers between devices  77.4 us (44%)
  starting transfers between devices  58.8 us (34%)
  Pallas kernels  18.1 us (10%)
  local copies, waits for them, and re-layouts  17.1 us (10%)
  other arithmetic  2.31 us (1%)
    ppermute x34, waiting for transfers between devices, swap(): return lax.ppermute(value, axis, [(i, i ^ distance) for i in range(count)])  77.4 us
    ppermute x34, starting transfers between devices, swap(): return lax.ppermute(value, axis, [(i, i ^ distance) for i in range(count)])  58.8 us
    pallas_call x4, Pallas kernels, blocked_dot(): pl.pallas_call(blocked_dot_kernel, grid_spec=spec, out_shape=[half, half]...  18.1 us
    dynamic_slice x5, local copies, waits for them, and re-layouts, piece(): lax.dynamic_slice(source, (span[0], (me ^ distance) * pairs), (span[1], p...  7.24 us
    unnamed x4, local copies, waits for them, and re-layouts  5.77 us
    broadcast_in_dim x1, local copies, waits for them, and re-layouts, local(): jnp.broadcast_to(irrep_ef.astype(jnp.bfloat16)[:, None], (pairs, LANES))  4 us
  transfers between devices with their start and end apart: 34, of which 10 were waited for; matrix products, arithmetic and copies ran while one was open for 7% of the time, Pallas kernels for 10%

profile of v2, /device:TPU:0, one launch (start us, length us, event | category | flops | bytes accessed | tf_op | source)
XLA Modules:
  0.0 174.1 jit_solution(10018310284059077996)
XLA Ops:
  0.0 0.9 constant_dynamic-slice_fusion.15
  0.9 6.1 %collective-permute-start.6 = (bf16[8,8192]{1,0:T(8,128)(2,1)S(1)}, bf16[8,8192]{1,0:T(8,128)(2,1)S(1)}, u32[]{:S(2)}, u32[]{:S(2)}) collective-permute-start(bf16[8,8192]{1,0:T(8,128)(2,1)S(1)} %constant_dynamic-slice_fusion.15), channel_id=1, source_target_pairs={{0,7},{1,6},{2,5},{3,4},{4,3},{5,2},{6,1},{7,0},{8,15},{9,14},{10,... | collective-permute-start | bytes 393224 | tf_op jit(solution)/shard_map/ppermute | solution.py:14
  7.0 1.3 constant_dynamic-slice_fusion.8
  8.4 1.8 %collective-permute-start.4 = (bf16[8,8192]{1,0:T(8,128)(2,1)S(1)}, bf16[8,8192]{1,0:T(8,128)(2,1)S(1)}, u32[]{:S(2)}, u32[]{:S(2)}) collective-permute-start(bf16[8,8192]{1,0:T(8,128)(2,1)S(1)} %get-tuple-element.30), channel_id=1, source_target_pairs={{0,6},{1,7},{2,4},{3,5},{4,2},{5,3},{6,0},{7,1},{8,14},{9,15},{10,... | collective-permute-start | bytes 393224 | tf_op jit(solution)/shard_map/ppermute | solution.py:14
  10.2 1.0 collective-permute-start.3
  11.3 1.9 %collective-permute-start.2 = (bf16[8,8192]{1,0:T(8,128)(2,1)S(1)}, bf16[8,8192]{1,0:T(8,128)(2,1)S(1)}, u32[]{:S(2)}, u32[]{:S(2)}) collective-permute-start(bf16[8,8192]{1,0:T(8,128)(2,1)S(1)} %get-tuple-element.32), channel_id=1, source_target_pairs={{0,3},{1,2},{2,1},{3,0},{4,7},{5,6},{6,5},{7,4},{8,11},{9,10},{10,... | collective-permute-start | bytes 393224 | tf_op jit(solution)/shard_map/ppermute | solution.py:14
  13.1 1.2 collective-permute-start.1
  14.3 10.3 %collective-permute-done.5.refs_6_ = bf16[8,8192]{1,0:T(8,128)(2,1)S(1)} collective-permute-done((bf16[8,8192]{1,0:T(8,128)(2,1)S(1)}, bf16[8,8192]{1,0:T(8,128)(2,1)S(1)}, u32[]{:S(2)}, u32[]{:S(2)}) %collective-permute-start.5) | collective-permute-done | bytes 131104 | tf_op jit(solution)/shard_map/ppermute | solution.py:14
  24.6 1.3 constant_dynamic-slice_fusion
  25.9 0.7 convert_element_type.7
  26.6 0.8 convert_element_type.6
  27.4 3.2 %collective-permute-start.16 = (bf16[16,8192]{1,0:T(8,128)(2,1)S(1)}, bf16[16,8192]{1,0:T(8,128)(2,1)S(1)}, u32[]{:S(2)}, u32[]{:S(2)}) collective-permute-start(bf16[16,8192]{1,0:T(8,128)(2,1)S(1)} %get-tuple-element.36), channel_id=1, source_target_pairs={{0,7},{1,6},{2,5},{3,4},{4,3},{5,2},{6,1},{7,0},{8,15},{9,14},{10,... | collective-permute-start | bytes 786440 | tf_op jit(solution)/shard_map/ppermute | solution.py:14
  30.6 1.1 collective-permute-start.15
  31.8 4.0 %broadcast_in_dim.4.refs_9_.refs_3_ = bf16[8192,128]{1,0:T(8,128)(2,1)S(1)} broadcast(bf16[8192]{0:T(1024)(128)(2,1)S(1)} %convert_element_type.6), dimensions={0} | broadcast | bytes 2113536 | tf_op jit(solution)/shard_map/broadcast_in_dim | solution.py:122
  35.8 5.8 %copy-done = bf16[8192,1024]{1,0:T(8,128)(2,1)S(1)} copy-done((bf16[8192,1024]{1,0:T(8,128)(2,1)S(1)}, bf16[8192,1024]{1,0:T(8,128)(2,1)}, u32[]{:S(2)}) %copy-start) | copy-done | bytes 16777240
  41.6 4.2 %shard_map.46 = (f32[128,256]{1,0:T(8,128)S(1)}, f32[128,256]{1,0:T(8,128)S(1)}) custom-call(s32[1]{0:T(128)} %bitcast.group, bf16[8,8192]{1,0:T(8,128)(2,1)S(1)} %get-tuple-element.35.refs_0_, bf16[8,8192]{1,0:T(8,128)(2,1)S(1)} %collective-permute-done.refs_1_, bf16[8,8192]{1,0:T(8,128)(2,1)S(1)} %collective-permute-done.1.refs_2_, ...), custom_call_target="tpu_custom_call" | custom-call | flops 1073741824 | bytes 16777216 | tf_op jit(solution)/shard_map/pallas_call | solution.py:77
  45.9 1.9 %constant_dynamic-slice_fusion.18 = (bf16[24,8192]{1,0:T(8,128)(2,1)S(1)}, bf16[24,8192]{1,0:T(8,128)(2,1)S(1)}, bf16[24,8192]{1,0:T(8,128)(2,1)S(1)}, bf16[24,8192]{1,0:T(8,128)(2,1)S(1)}) fusion(bf16[48,65536]{1,0:T(8,128)(2,1)} %param.4, s32[]{:T(128)S(6)} %select_n.16, s32[]{:T(128)S(6)} %select_n.43, s32[]{:T(128)S(6)} %select_n.41, s32[]{:T(128)S(6)} %select_n.42), kind=kLoop, calls=%fused_computation.30 | loop fusion | bytes 3145744 | tf_op jit(solution)/shard_map/dynamic_slice | solution.py:136
  47.8 4.2 %collective-permute-start.29 = (bf16[24,8192]{1,0:T(8,128)(2,1)S(1)}, bf16[24,8192]{1,0:T(8,128)(2,1)S(1)}, u32[]{:S(2)}, u32[]{:S(2)}) collective-permute-start(bf16[24,8192]{1,0:T(8,128)(2,1)S(1)} %get-tuple-element.26), channel_id=1, source_target_pairs={{0,5},{1,4},{2,7},{3,6},{4,1},{5,0},{6,3},{7,2},{8,13},{9,12},{10,... | collective-permute-start | bytes 1179656 | tf_op jit(solution)/shard_map/ppermute | solution.py:14
  52.0 2.0 %collective-permute-start.28 = (bf16[24,8192]{1,0:T(8,128)(2,1)S(1)}, bf16[24,8192]{1,0:T(8,128)(2,1)S(1)}, u32[]{:S(2)}, u32[]{:S(2)}) collective-permute-start(bf16[24,8192]{1,0:T(8,128)(2,1)S(1)} %get-tuple-element.27), channel_id=1, source_target_pairs={{0,4},{1,5},{2,6},{3,7},{4,0},{5,1},{6,2},{7,3},{8,12},{9,13},{10,... | collective-permute-start | bytes 1179656 | tf_op jit(solution)/shard_map/ppermute | solution.py:14
  54.1 1.6 collective-permute-start.8
  55.6 1.9 %constant_dynamic-slice_fusion.4 = (bf16[40,8192]{1,0:T(8,128)(2,1)S(1)}, bf16[40,8192]{1,0:T(8,128)(2,1)S(1)}, bf16[40,8192]{1,0:T(8,128)(2,1)S(1)}, bf16[40,8192]{1,0:T(8,128)(2,1)S(1)}) fusion(bf16[48,65536]{1,0:T(8,128)(2,1)} %param.4, s32[]{:T(128)S(6)} %select_n.40, s32[]{:T(128)S(6)} %select_n.19, s32[]{:T(128)S(6)} %select_n.18, s32[]{:T(128)S(6)} %select_n.17), kind=kLoop, calls=%fused_computation.16 | loop fusion | bytes 5242896 | tf_op jit(solution)/shard_map/dynamic_slice | solution.py:136
  57.5 0.7 collective-permute-start.12
  58.2 1.4 collective-permute-start.11
  59.6 1.4 collective-permute-start.10
  61.1 17.9 %collective-permute-done.29.refs_1_ = bf16[24,8192]{1,0:T(8,128)(2,1)S(1)} collective-permute-done((bf16[24,8192]{1,0:T(8,128)(2,1)S(1)}, bf16[24,8192]{1,0:T(8,128)(2,1)S(1)}, u32[]{:S(2)}, u32[]{:S(2)}) %collective-permute-start.29) | collective-permute-done | bytes 393248 | tf_op jit(solution)/shard_map/ppermute | solution.py:14
  78.9 2.4 %collective-permute-start.14 = (bf16[16,8192]{1,0:T(8,128)(2,1)S(1)}, bf16[16,8192]{1,0:T(8,128)(2,1)S(1)}, u32[]{:S(2)}, u32[]{:S(2)}) collective-permute-start(bf16[16,8192]{1,0:T(8,128)(2,1)S(1)} %get-tuple-element.38), channel_id=1, source_target_pairs={{0,6},{1,7},{2,4},{3,5},{4,2},{5,3},{6,0},{7,1},{8,14},{9,15},{10,... | collective-permute-start | bytes 786440 | tf_op jit(solution)/shard_map/ppermute | solution.py:14
  81.3 6.4 %collective-permute-done.28.refs_0_ = bf16[24,8192]{1,0:T(8,128)(2,1)S(1)} collective-permute-done((bf16[24,8192]{1,0:T(8,128)(2,1)S(1)}, bf16[24,8192]{1,0:T(8,128)(2,1)S(1)}, u32[]{:S(2)}, u32[]{:S(2)}) %collective-permute-start.28) | collective-permute-done | bytes 393248 | tf_op jit(solution)/shard_map/ppermute | solution.py:14
  87.7 4.2 %shard_map.49 = (f32[96,256]{1,0:T(8,128)S(1)}, f32[96,256]{1,0:T(8,128)S(1)}) custom-call(s32[1]{0:T(128)} %bitcast.group, bf16[24,8192]{1,0:T(8,128)(2,1)S(1)} %collective-permute-done.28.refs_0_, bf16[24,8192]{1,0:T(8,128)(2,1)S(1)} %collective-permute-done.29.refs_1_, bf16[8192,1024]{1,0:T(8,128)(2,1)S(1)} %copy-done.1, ...), custom_call_target="tpu_custom_call" | custom-call | flops 805306368 | bytes 16777216 | tf_op jit(solution)/shard_map/pallas_call | solution.py:77
  91.9 13.4 %collective-permute-done.14.refs_5_ = bf16[16,8192]{1,0:T(8,128)(2,1)S(1)} collective-permute-done((bf16[16,8192]{1,0:T(8,128)(2,1)S(1)}, bf16[16,8192]{1,0:T(8,128)(2,1)S(1)}, u32[]{:S(2)}, u32[]{:S(2)}) %collective-permute-start.14) | collective-permute-done | bytes 262176 | tf_op jit(solution)/shard_map/ppermute | solution.py:14
  105.2 2.0 %collective-permute-start.23 = (bf16[24,8192]{1,0:T(8,128)(2,1)S(1)}, bf16[24,8192]{1,0:T(8,128)(2,1)S(1)}, u32[]{:S(2)}, u32[]{:S(2)}) collective-permute-start(bf16[24,8192]{1,0:T(8,128)(2,1)S(1)} %get-tuple-element.25), channel_id=1, source_target_pairs={{0,7},{1,6},{2,5},{3,4},{4,3},{5,2},{6,1},{7,0},{8,15},{9,14},{10,... | collective-permute-start | bytes 1179656 | tf_op jit(solution)/shard_map/ppermute | solution.py:14
  107.2 2.2 %collective-permute-done.13.refs_4_ = bf16[16,8192]{1,0:T(8,128)(2,1)S(1)} collective-permute-done((bf16[16,8192]{1,0:T(8,128)(2,1)S(1)}, bf16[16,8192]{1,0:T(8,128)(2,1)S(1)}, u32[]{:S(2)}, u32[]{:S(2)}) %collective-permute-start.13) | collective-permute-done | bytes 262176 | tf_op jit(solution)/shard_map/ppermute | solution.py:14
  109.4 0.9 collective-permute-start.22
  110.3 1.8 %collective-permute-start.9 = (f32[32,256]{1,0:T(8,128)S(1)}, f32[32,256]{1,0:T(8,128)S(1)}, u32[]{:S(2)}, u32[]{:S(2)}) collective-permute-start(f32[32,256]{1,0:T(8,128)S(1)} %pad_maximum_fusion.2), channel_id=1, source_target_pairs={{0,1},{1,0},{2,3},{3,2},{4,5},{5,4},{6,7},{7,6},{8,9},{9,8},{10,11... | collective-permute-start | bytes 98312 | tf_op jit(solution)/shard_map/ppermute | solution.py:14
  112.1 19.4 %collective-permute-done.10.refs_1_ = bf16[40,8192]{1,0:T(8,128)(2,1)S(1)} collective-permute-done((bf16[40,8192]{1,0:T(8,128)(2,1)S(1)}, bf16[40,8192]{1,0:T(8,128)(2,1)S(1)}, u32[]{:S(2)}, u32[]{:S(2)}) %collective-permute-start.10) | collective-permute-done | bytes 655392 | tf_op jit(solution)/shard_map/ppermute | solution.py:14
  131.4 5.6 %shard_map.47 = (f32[448,256]{1,0:T(8,128)S(1)}, f32[448,256]{1,0:T(8,128)S(1)}) custom-call(s32[1]{0:T(128)} %bitcast.group, bf16[40,8192]{1,0:T(8,128)(2,1)S(1)} %get-tuple-element.43.refs_0_, bf16[40,8192]{1,0:T(8,128)(2,1)S(1)} %collective-permute-done.10.refs_1_, bf16[40,8192]{1,0:T(8,128)(2,1)S(1)} %collective-permute-done.11.refs_2_, ...), custom_call_target="tpu_custom_call" | custom-call | flops 3758096384 | bytes 16777216 | tf_op jit(solution)/shard_map/pallas_call | solution.py:77
  137.2 4.2 %shard_map.48 = (f32[96,256]{1,0:T(8,128)S(1)}, f32[96,256]{1,0:T(8,128)S(1)}) custom-call(s32[1]{0:T(128)} %bitcast.group, bf16[24,8192]{1,0:T(8,128)(2,1)S(1)} %collective-permute-done.22.refs_0_, bf16[24,8192]{1,0:T(8,128)(2,1)S(1)} %collective-permute-done.23.refs_1_, bf16[8192,1024]{1,0:T(8,128)(2,1)S(1)} %copy-done.1, ...), custom_call_target="tpu_custom_call" | custom-call | flops 805306368 | bytes 16777216 | tf_op jit(solution)/shard_map/pallas_call | solution.py:77
  142.9 1.3 collective-permute-start.25
  144.2 0.9 collective-permute-start.18
  145.1 1.2 collective-permute-done.31
  146.3 7.1 %collective-permute-start.32 = (f32[24,256]{1,0:T(8,128)S(1)}, f32[24,256]{1,0:T(8,128)S(1)}, u32[]{:S(2)}, u32[]{:S(2)}) collective-permute-start(f32[24,256]{1,0:T(8,128)S(1)} %get-tuple-element.58), channel_id=1, source_target_pairs={{0,5},{1,4},{2,7},{3,6},{4,1},{5,0},{6,3},{7,2},{8,13},{9,12},{10,... | collective-permute-start | bytes 73736 | tf_op jit(solution)/shard_map/ppermute | solution.py:14
  153.4 0.7 collective-permute-start.33
  154.2 1.5 collective-permute-start.19
  155.7 3.4 %collective-permute-done.19 = f32[112,256]{1,0:T(8,128)S(1)} collective-permute-done((f32[112,256]{1,0:T(8,128)S(1)}, f32[112,256]{1,0:T(8,128)S(1)}, u32[]{:S(2)}, u32[]{:S(2)}) %collective-permute-start.19) | collective-permute-done | bytes 114720 | tf_op jit(solution)/shard_map/ppermute | solution.py:14
  159.1 5.2 %collective-permute-start.20 = (f32[72,256]{1,0:T(8,128)S(1)}, f32[72,256]{1,0:T(8,128)S(1)}, u32[]{:S(2)}, u32[]{:S(2)}) collective-permute-start(f32[72,256]{1,0:T(8,128)S(1)} %pad_maximum_fusion.1), channel_id=1, source_target_pairs={{0,2},{1,3},{2,0},{3,1},{4,6},{5,7},{6,4},{7,5},{8,10},{9,11},{10,... | collective-permute-start | bytes 221192 | tf_op jit(solution)/shard_map/ppermute | solution.py:14
  164.4 2.6 %collective-permute-start.27 = (f32[24,256]{1,0:T(8,128)S(1)}, f32[24,256]{1,0:T(8,128)S(1)}, u32[]{:S(2)}, u32[]{:S(2)}) collective-permute-start(f32[24,256]{1,0:T(8,128)S(1)} %get-tuple-element.56), channel_id=1, source_target_pairs={{0,6},{1,7},{2,4},{3,5},{4,2},{5,3},{6,0},{7,1},{8,14},{9,15},{10,... | collective-permute-start | bytes 73736 | tf_op jit(solution)/shard_map/ppermute | solution.py:14
  167.0 0.7 collective-permute-start.26
  167.7 2.8 %collective-permute-start.21 = (f32[24,256]{1,0:T(8,128)S(1)}, f32[24,256]{1,0:T(8,128)S(1)}, u32[]{:S(2)}, u32[]{:S(2)}) collective-permute-start(f32[24,256]{1,0:T(8,128)S(1)} %concatenate.37), channel_id=1, source_target_pairs={{0,4},{1,5},{2,6},{3,7},{4,0},{5,1},{6,2},{7,3},{8,12},{9,13},{10,... | collective-permute-start | bytes 73736 | tf_op jit(solution)/shard_map/ppermute | solution.py:14
  170.5 3.0 %collective-permute-done.26 = f32[24,256]{1,0:T(8,128)S(1)} collective-permute-done((f32[24,256]{1,0:T(8,128)S(1)}, f32[24,256]{1,0:T(8,128)S(1)}, u32[]{:S(2)}, u32[]{:S(2)}) %collective-permute-start.26) | collective-permute-done | bytes 24608 | tf_op jit(solution)/shard_map/ppermute | solution.py:14
  (66 shorter events, 2.7 us)
Async XLA Ops:
  0.9 12.2 %collective-permute-start.6 = (bf16[8,8192]{1,0:T(8,128)(2,1)S(1)}, bf16[8,8192]{1,0:T(8,128)(2,1)S(1)}, u32[]{:S(2)}, u32[]{:S(2)}) collective-permute-start(bf16[8,8192]{1,0:T(8,128)(2,1)S(1)} %constant_dynamic-slice_fusion.15), channel_id=1, source_target_pairs={{0,7},{1,6},{2,5},{3,4},{4,3},{5,2},{6,1},{7,0},{8,15},{9,14},{10,... | collective-permute-start | bytes 393224 | tf_op jit(solution)/shard_map/ppermute | solution.py:14
  8.3 16.3 %collective-permute-start.5 = (bf16[8,8192]{1,0:T(8,128)(2,1)S(1)}, bf16[8,8192]{1,0:T(8,128)(2,1)S(1)}, u32[]{:S(2)}, u32[]{:S(2)}) collective-permute-start(bf16[8,8192]{1,0:T(8,128)(2,1)S(1)} %get-tuple-element.29), channel_id=1, source_target_pairs={{0,5},{1,4},{2,7},{3,6},{4,1},{5,0},{6,3},{7,2},{8,13},{9,12},{10,... | collective-permute-start | bytes 393224 | tf_op jit(solution)/shard_map/ppermute | solution.py:14
  8.4 19.0 %collective-permute-start.4 = (bf16[8,8192]{1,0:T(8,128)(2,1)S(1)}, bf16[8,8192]{1,0:T(8,128)(2,1)S(1)}, u32[]{:S(2)}, u32[]{:S(2)}) collective-permute-start(bf16[8,8192]{1,0:T(8,128)(2,1)S(1)} %get-tuple-element.30), channel_id=1, source_target_pairs={{0,6},{1,7},{2,4},{3,5},{4,2},{5,3},{6,0},{7,1},{8,14},{9,15},{10,... | collective-permute-start | bytes 393224 | tf_op jit(solution)/shard_map/ppermute | solution.py:14
  10.2 20.4 %collective-permute-start.3 = (bf16[8,8192]{1,0:T(8,128)(2,1)S(1)}, bf16[8,8192]{1,0:T(8,128)(2,1)S(1)}, u32[]{:S(2)}, u32[]{:S(2)}) collective-permute-start(bf16[8,8192]{1,0:T(8,128)(2,1)S(1)} %get-tuple-element.31), channel_id=1, source_target_pairs={{0,4},{1,5},{2,6},{3,7},{4,0},{5,1},{6,2},{7,3},{8,12},{9,13},{10,... | collective-permute-start | bytes 393224 | tf_op jit(solution)/shard_map/ppermute | solution.py:14
  11.3 20.5 %collective-permute-start.2 = (bf16[8,8192]{1,0:T(8,128)(2,1)S(1)}, bf16[8,8192]{1,0:T(8,128)(2,1)S(1)}, u32[]{:S(2)}, u32[]{:S(2)}) collective-permute-start(bf16[8,8192]{1,0:T(8,128)(2,1)S(1)} %get-tuple-element.32), channel_id=1, source_target_pairs={{0,3},{1,2},{2,1},{3,0},{4,7},{5,6},{6,5},{7,4},{8,11},{9,10},{10,... | collective-permute-start | bytes 393224 | tf_op jit(solution)/shard_map/ppermute | solution.py:14
  13.1 18.7 %collective-permute-start.1 = (bf16[8,8192]{1,0:T(8,128)(2,1)S(1)}, bf16[8,8192]{1,0:T(8,128)(2,1)S(1)}, u32[]{:S(2)}, u32[]{:S(2)}) collective-permute-start(bf16[8,8192]{1,0:T(8,128)(2,1)S(1)} %get-tuple-element.33), channel_id=1, source_target_pairs={{0,1},{1,0},{2,3},{3,2},{4,5},{5,4},{6,7},{7,6},{8,9},{9,8},{10,11... | collective-permute-start | bytes 393224 | tf_op jit(solution)/shard_map/ppermute | solution.py:14
  24.6 7.1 %collective-permute-start = (bf16[8,8192]{1,0:T(8,128)(2,1)S(1)}, bf16[8,8192]{1,0:T(8,128)(2,1)S(1)}, u32[]{:S(2)}, u32[]{:S(2)}) collective-permute-start(bf16[8,8192]{1,0:T(8,128)(2,1)S(1)} %get-tuple-element.34), channel_id=1, source_target_pairs={{0,2},{1,3},{2,0},{3,1},{4,6},{5,7},{6,4},{7,5},{8,10},{9,11},{10,... | collective-permute-start | bytes 393224 | tf_op jit(solution)/shard_map/ppermute | solution.py:14
  27.4 30.1 %collective-permute-start.16 = (bf16[16,8192]{1,0:T(8,128)(2,1)S(1)}, bf16[16,8192]{1,0:T(8,128)(2,1)S(1)}, u32[]{:S(2)}, u32[]{:S(2)}) collective-permute-start(bf16[16,8192]{1,0:T(8,128)(2,1)S(1)} %get-tuple-element.36), channel_id=1, source_target_pairs={{0,7},{1,6},{2,5},{3,4},{4,3},{5,2},{6,1},{7,0},{8,15},{9,14},{10,... | collective-permute-start | bytes 786440 | tf_op jit(solution)/shard_map/ppermute | solution.py:14
  30.6 27.6 %collective-permute-start.15 = (bf16[16,8192]{1,0:T(8,128)(2,1)S(1)}, bf16[16,8192]{1,0:T(8,128)(2,1)S(1)}, u32[]{:S(2)}, u32[]{:S(2)}) collective-permute-start(bf16[16,8192]{1,0:T(8,128)(2,1)S(1)} %get-tuple-element.37), channel_id=1, source_target_pairs={{0,5},{1,4},{2,7},{3,6},{4,1},{5,0},{6,3},{7,2},{8,13},{9,12},{10,... | collective-permute-start | bytes 786440 | tf_op jit(solution)/shard_map/ppermute | solution.py:14
  35.8 5.8 %copy-start = (bf16[8192,1024]{1,0:T(8,128)(2,1)S(1)}, bf16[8192,1024]{1,0:T(8,128)(2,1)}, u32[]{:S(2)}) copy-start(bf16[8192,1024]{1,0:T(8,128)(2,1)} %refs_2_.3) | copy-start | bytes 50331652
  41.6 46.1 %copy-start.1 = (bf16[8192,1024]{1,0:T(8,128)(2,1)S(1)}, bf16[8192,1024]{1,0:T(8,128)(2,1)}, u32[]{:S(2)}) copy-start(bf16[8192,1024]{1,0:T(8,128)(2,1)} %refs_2_.3) | copy-start | bytes 50331652
  45.8 8.2 %collective-permute-start.7 = (f32[128,256]{1,0:T(8,128)S(1)}, f32[128,256]{1,0:T(8,128)S(1)}, u32[]{:S(2)}, u32[]{:S(2)}) collective-permute-start(f32[128,256]{1,0:T(8,128)S(1)} %get-tuple-element.18), channel_id=1, source_target_pairs={{0,8},{8,0},{16,24},{24,16},{1,9},{9,1},{17,25},{25,17},{2,10},{10... | collective-permute-start | bytes 393224 | tf_op jit(solution)/shard_map/ppermute | solution.py:14
  47.8 31.1 %collective-permute-start.29 = (bf16[24,8192]{1,0:T(8,128)(2,1)S(1)}, bf16[24,8192]{1,0:T(8,128)(2,1)S(1)}, u32[]{:S(2)}, u32[]{:S(2)}) collective-permute-start(bf16[24,8192]{1,0:T(8,128)(2,1)S(1)} %get-tuple-element.26), channel_id=1, source_target_pairs={{0,5},{1,4},{2,7},{3,6},{4,1},{5,0},{6,3},{7,2},{8,13},{9,12},{10,... | collective-permute-start | bytes 1179656 | tf_op jit(solution)/shard_map/ppermute | solution.py:14
  52.0 35.7 %collective-permute-start.28 = (bf16[24,8192]{1,0:T(8,128)(2,1)S(1)}, bf16[24,8192]{1,0:T(8,128)(2,1)S(1)}, u32[]{:S(2)}, u32[]{:S(2)}) collective-permute-start(bf16[24,8192]{1,0:T(8,128)(2,1)S(1)} %get-tuple-element.27), channel_id=1, source_target_pairs={{0,4},{1,5},{2,6},{3,7},{4,0},{5,1},{6,2},{7,3},{8,12},{9,13},{10,... | collective-permute-start | bytes 1179656 | tf_op jit(solution)/shard_map/ppermute | solution.py:14
  54.1 5.6 %collective-permute-start.8 = (f32[64,256]{1,0:T(8,128)S(1)}, f32[64,256]{1,0:T(8,128)S(1)}, u32[]{:S(2)}, u32[]{:S(2)}) collective-permute-start(f32[64,256]{1,0:T(8,128)S(1)} %slice.143), channel_id=1, source_target_pairs={{0,16},{8,24},{16,0},{24,8},{1,17},{9,25},{17,1},{25,9},{2,18},{10... | collective-permute-start | bytes 196616 | tf_op jit(solution)/shard_map/ppermute | solution.py:14
  57.5 52.8 %collective-permute-start.12 = (bf16[40,8192]{1,0:T(8,128)(2,1)S(1)}, bf16[40,8192]{1,0:T(8,128)(2,1)S(1)}, u32[]{:S(2)}, u32[]{:S(2)}) collective-permute-start(bf16[40,8192]{1,0:T(8,128)(2,1)S(1)} %get-tuple-element.40), channel_id=1, source_target_pairs={{0,3},{1,2},{2,1},{3,0},{4,7},{5,6},{6,5},{7,4},{8,11},{9,10},{10,... | collective-permute-start | bytes 1966088 | tf_op jit(solution)/shard_map/ppermute | solution.py:14
  58.2 53.8 %collective-permute-start.11 = (bf16[40,8192]{1,0:T(8,128)(2,1)S(1)}, bf16[40,8192]{1,0:T(8,128)(2,1)S(1)}, u32[]{:S(2)}, u32[]{:S(2)}) collective-permute-start(bf16[40,8192]{1,0:T(8,128)(2,1)S(1)} %get-tuple-element.41), channel_id=1, source_target_pairs={{0,1},{1,0},{2,3},{3,2},{4,5},{5,4},{6,7},{7,6},{8,9},{9,8},{10,11... | collective-permute-start | bytes 1966088 | tf_op jit(solution)/shard_map/ppermute | solution.py:14
  59.6 71.8 %collective-permute-start.10 = (bf16[40,8192]{1,0:T(8,128)(2,1)S(1)}, bf16[40,8192]{1,0:T(8,128)(2,1)S(1)}, u32[]{:S(2)}, u32[]{:S(2)}) collective-permute-start(bf16[40,8192]{1,0:T(8,128)(2,1)S(1)} %get-tuple-element.42), channel_id=1, source_target_pairs={{0,2},{1,3},{2,0},{3,1},{4,6},{5,7},{6,4},{7,5},{8,10},{9,11},{10,... | collective-permute-start | bytes 1966088 | tf_op jit(solution)/shard_map/ppermute | solution.py:14
  78.9 26.3 %collective-permute-start.14 = (bf16[16,8192]{1,0:T(8,128)(2,1)S(1)}, bf16[16,8192]{1,0:T(8,128)(2,1)S(1)}, u32[]{:S(2)}, u32[]{:S(2)}) collective-permute-start(bf16[16,8192]{1,0:T(8,128)(2,1)S(1)} %get-tuple-element.38), channel_id=1, source_target_pairs={{0,6},{1,7},{2,4},{3,5},{4,2},{5,3},{6,0},{7,1},{8,14},{9,15},{10,... | collective-permute-start | bytes 786440 | tf_op jit(solution)/shard_map/ppermute | solution.py:14
  87.7 21.7 %collective-permute-start.13 = (bf16[16,8192]{1,0:T(8,128)(2,1)S(1)}, bf16[16,8192]{1,0:T(8,128)(2,1)S(1)}, u32[]{:S(2)}, u32[]{:S(2)}) collective-permute-start(bf16[16,8192]{1,0:T(8,128)(2,1)S(1)} %get-tuple-element.39), channel_id=1, source_target_pairs={{0,4},{1,5},{2,6},{3,7},{4,0},{5,1},{6,2},{7,3},{8,12},{9,13},{10,... | collective-permute-start | bytes 786440 | tf_op jit(solution)/shard_map/ppermute | solution.py:14
  105.2 31.9 %collective-permute-start.23 = (bf16[24,8192]{1,0:T(8,128)(2,1)S(1)}, bf16[24,8192]{1,0:T(8,128)(2,1)S(1)}, u32[]{:S(2)}, u32[]{:S(2)}) collective-permute-start(bf16[24,8192]{1,0:T(8,128)(2,1)S(1)} %get-tuple-element.25), channel_id=1, source_target_pairs={{0,7},{1,6},{2,5},{3,4},{4,3},{5,2},{6,1},{7,0},{8,15},{9,14},{10,... | collective-permute-start | bytes 1179656 | tf_op jit(solution)/shard_map/ppermute | solution.py:14
  109.4 27.8 %collective-permute-start.22 = (bf16[24,8192]{1,0:T(8,128)(2,1)S(1)}, bf16[24,8192]{1,0:T(8,128)(2,1)S(1)}, u32[]{:S(2)}, u32[]{:S(2)}) collective-permute-start(bf16[24,8192]{1,0:T(8,128)(2,1)S(1)} %get-tuple-element.28), channel_id=1, source_target_pairs={{0,6},{1,7},{2,4},{3,5},{4,2},{5,3},{6,0},{7,1},{8,14},{9,15},{10,... | collective-permute-start | bytes 1179656 | tf_op jit(solution)/shard_map/ppermute | solution.py:14
  110.3 26.8 %collective-permute-start.9 = (f32[32,256]{1,0:T(8,128)S(1)}, f32[32,256]{1,0:T(8,128)S(1)}, u32[]{:S(2)}, u32[]{:S(2)}) collective-permute-start(f32[32,256]{1,0:T(8,128)S(1)} %pad_maximum_fusion.2), channel_id=1, source_target_pairs={{0,1},{1,0},{2,3},{3,2},{4,5},{5,4},{6,7},{7,6},{8,9},{9,8},{10,11... | collective-permute-start | bytes 98312 | tf_op jit(solution)/shard_map/ppermute | solution.py:14
  112.1 29.8 %collective-permute-start.30 = (f32[96,256]{1,0:T(8,128)S(1)}, f32[96,256]{1,0:T(8,128)S(1)}, u32[]{:S(2)}, u32[]{:S(2)}) collective-permute-start(f32[96,256]{1,0:T(8,128)S(1)} %get-tuple-element.24), channel_id=1, source_target_pairs={{0,8},{8,0},{16,24},{24,16},{1,9},{9,1},{17,25},{25,17},{2,10},{10... | collective-permute-start | bytes 294920 | tf_op jit(solution)/shard_map/ppermute | solution.py:14
  137.0 7.1 %collective-permute-start.17 = (f32[448,256]{1,0:T(8,128)S(1)}, f32[448,256]{1,0:T(8,128)S(1)}, u32[]{:S(2)}, u32[]{:S(2)}) collective-permute-start(f32[448,256]{1,0:T(8,128)S(1)} %get-tuple-element.20), channel_id=1, source_target_pairs={{0,8},{8,0},{16,24},{24,16},{1,9},{9,1},{17,25},{25,17},{2,10},{10... | collective-permute-start | bytes 1376264 | tf_op jit(solution)/shard_map/ppermute | solution.py:14
  141.3 1.5 collective-permute-start.24
  141.9 4.4 %collective-permute-start.31 = (f32[48,256]{1,0:T(8,128)S(1)}, f32[48,256]{1,0:T(8,128)S(1)}, u32[]{:S(2)}, u32[]{:S(2)}) collective-permute-start(f32[48,256]{1,0:T(8,128)S(1)} %slice.167), channel_id=1, source_target_pairs={{0,16},{8,24},{16,0},{24,8},{1,17},{9,25},{17,1},{25,9},{2,18},{10... | collective-permute-start | bytes 147464 | tf_op jit(solution)/shard_map/ppermute | solution.py:14
  142.9 12.8 %collective-permute-start.25 = (f32[48,256]{1,0:T(8,128)S(1)}, f32[48,256]{1,0:T(8,128)S(1)}, u32[]{:S(2)}, u32[]{:S(2)}) collective-permute-start(f32[48,256]{1,0:T(8,128)S(1)} %slice.163), channel_id=1, source_target_pairs={{0,16},{8,24},{16,0},{24,8},{1,17},{9,25},{17,1},{25,9},{2,18},{10... | collective-permute-start | bytes 147464 | tf_op jit(solution)/shard_map/ppermute | solution.py:14
  144.2 9.9 %collective-permute-start.18 = (f32[224,256]{1,0:T(8,128)S(1)}, f32[224,256]{1,0:T(8,128)S(1)}, u32[]{:S(2)}, u32[]{:S(2)}) collective-permute-start(f32[224,256]{1,0:T(8,128)S(1)} %slice.150), channel_id=1, source_target_pairs={{0,16},{8,24},{16,0},{24,8},{1,17},{9,25},{17,1},{25,9},{2,18},{10... | collective-permute-start | bytes 688136 | tf_op jit(solution)/shard_map/ppermute | solution.py:14
  146.3 24.2 %collective-permute-start.32 = (f32[24,256]{1,0:T(8,128)S(1)}, f32[24,256]{1,0:T(8,128)S(1)}, u32[]{:S(2)}, u32[]{:S(2)}) collective-permute-start(f32[24,256]{1,0:T(8,128)S(1)} %get-tuple-element.58), channel_id=1, source_target_pairs={{0,5},{1,4},{2,7},{3,6},{4,1},{5,0},{6,3},{7,2},{8,13},{9,12},{10,... | collective-permute-start | bytes 73736 | tf_op jit(solution)/shard_map/ppermute | solution.py:14
  153.4 17.0 %collective-permute-start.33 = (f32[24,256]{1,0:T(8,128)S(1)}, f32[24,256]{1,0:T(8,128)S(1)}, u32[]{:S(2)}, u32[]{:S(2)}) collective-permute-start(f32[24,256]{1,0:T(8,128)S(1)} %get-tuple-element.59), channel_id=1, source_target_pairs={{0,4},{1,5},{2,6},{3,7},{4,0},{5,1},{6,2},{7,3},{8,12},{9,13},{10,... | collective-permute-start | bytes 73736 | tf_op jit(solution)/shard_map/ppermute | solution.py:14
  154.2 4.9 %collective-permute-start.19 = (f32[112,256]{1,0:T(8,128)S(1)}, f32[112,256]{1,0:T(8,128)S(1)}, u32[]{:S(2)}, u32[]{:S(2)}) collective-permute-start(f32[112,256]{1,0:T(8,128)S(1)} %pad_maximum_fusion), channel_id=1, source_target_pairs={{0,1},{1,0},{2,3},{3,2},{4,5},{5,4},{6,7},{7,6},{8,9},{9,8},{10,11... | collective-permute-start | bytes 344072 | tf_op jit(solution)/shard_map/ppermute | solution.py:14
  159.1 8.5 %collective-permute-start.20 = (f32[72,256]{1,0:T(8,128)S(1)}, f32[72,256]{1,0:T(8,128)S(1)}, u32[]{:S(2)}, u32[]{:S(2)}) collective-permute-start(f32[72,256]{1,0:T(8,128)S(1)} %pad_maximum_fusion.1), channel_id=1, source_target_pairs={{0,2},{1,3},{2,0},{3,1},{4,6},{5,7},{6,4},{7,5},{8,10},{9,11},{10,... | collective-permute-start | bytes 221192 | tf_op jit(solution)/shard_map/ppermute | solution.py:14
  164.4 6.1 %collective-permute-start.27 = (f32[24,256]{1,0:T(8,128)S(1)}, f32[24,256]{1,0:T(8,128)S(1)}, u32[]{:S(2)}, u32[]{:S(2)}) collective-permute-start(f32[24,256]{1,0:T(8,128)S(1)} %get-tuple-element.56), channel_id=1, source_target_pairs={{0,6},{1,7},{2,4},{3,5},{4,2},{5,3},{6,0},{7,1},{8,14},{9,15},{10,... | collective-permute-start | bytes 73736 | tf_op jit(solution)/shard_map/ppermute | solution.py:14
  167.0 6.5 %collective-permute-start.26 = (f32[24,256]{1,0:T(8,128)S(1)}, f32[24,256]{1,0:T(8,128)S(1)}, u32[]{:S(2)}, u32[]{:S(2)}) collective-permute-start(f32[24,256]{1,0:T(8,128)S(1)} %get-tuple-element.57), channel_id=1, source_target_pairs={{0,7},{1,6},{2,5},{3,4},{4,3},{5,2},{6,1},{7,0},{8,15},{9,14},{10,... | collective-permute-start | bytes 73736 | tf_op jit(solution)/shard_map/ppermute | solution.py:14
  167.7 5.8 %collective-permute-start.21 = (f32[24,256]{1,0:T(8,128)S(1)}, f32[24,256]{1,0:T(8,128)S(1)}, u32[]{:S(2)}, u32[]{:S(2)}) collective-permute-start(f32[24,256]{1,0:T(8,128)S(1)} %concatenate.37), channel_id=1, source_target_pairs={{0,4},{1,5},{2,6},{3,7},{4,0},{5,1},{6,2},{7,3},{8,12},{9,13},{10,... | collective-permute-start | bytes 73736 | tf_op jit(solution)/shard_map/ppermute | solution.py:14

commit v3 on v0

v3 whole, which is shorter than its diff:
```python
import functools

import jax
import jax.numpy as jnp
from jax import lax
from jax.experimental import pallas as pl
from jax.experimental.pallas import tpu as pltpu
from jax.sharding import PartitionSpec as P

SHARES = (1, 2, 3)
LANES = 128


def swap(value, axis, distance):
    count = lax.axis_size(axis)
    return lax.ppermute(value, axis, [(i, i ^ distance) for i in range(count)])


def reversed_bits(count):
    levels = count.bit_length() - 1
    return [sum(((p >> i) & 1) << (levels - 1 - i) for i in range(levels)) for p in range(count)]


def row_chunks(rows):
    if rows % (8 * sum(SHARES)):
        return [rows]
    unit = rows // sum(SHARES)
    return [share * unit for share in SHARES]


def product_kernel(blocks, group, *refs):
    pieces, values, out = refs[:-2], refs[-2], refs[-1]
    rows, width = out.shape[0] // len(blocks), out.shape[1]
    pairs = values.shape[0]
    slab = next(s for s in (1024, 512, 256, 128, pairs) if pairs % s == 0)
    for k in range(pairs // slab):
        at = slice(k * slab, (k + 1) * slab)
        left = jnp.concatenate([piece[:, at] for piece in pieces], 0)
        for i, j in enumerate(blocks):
            start = pl.multiple_of((group[0] ^ j) * width, LANES)
            right = values[at, pl.ds(start, width)]
            term = jnp.dot(left, right, preferred_element_type=jnp.float32)
            rest = slice(i * rows, (i + 1) * rows)
            out[rest, :] = term if k == 0 else out[rest, :] + term


def product(pieces, values, group, groups, blocks):
    pairs, columns = values.shape
    rows = sum(piece.shape[0] for piece in pieces)
    out = jax.ShapeDtypeStruct((rows * len(blocks), columns // groups), jnp.float32)
    whole = pl.BlockSpec(memory_space=pltpu.VMEM)
    return pl.pallas_call(
        functools.partial(product_kernel, blocks),
        in_specs=[pl.BlockSpec(memory_space=pltpu.SMEM)] + [whole] * (len(pieces) + 1),
        out_specs=whole,
        out_shape=out,
        cost_estimate=pl.CostEstimate(
            flops=2 * pairs * out.shape[0] * out.shape[1],
            bytes_accessed=2 * pairs * columns * len(blocks) // groups,
            transcendentals=0,
        ),
        compiler_params=pltpu.CompilerParams(vmem_limit_bytes=12 << 20),
    )(group, *pieces, values)


def columns_to_owner(pieces, product_of, groups):
    rows = sum(piece.shape[0] for piece in pieces)
    came = {j: [] for j in range(groups)}

    def term(blocks):
        return product_of(pieces, blocks)

    bit = 1
    while bit < groups:
        blocks = range(bit, groups, 2 * bit)
        out = term(blocks)
        if came[bit]:
            out = out + sum(jnp.concatenate(parts, 0) for parts in zip(*[came[j] for j in blocks]))
        got = cut(swap(out, "grp", bit), [rows] * len(blocks))
        for j, part in zip(blocks, got):
            came[j - bit].append(part)
        bit *= 2
    out = term([0])
    return out + sum(came[0])


def fold(shares, distance):
    halves = [share.shape[0] // 2 for share in shares]
    out = jnp.concatenate([share[h:] for share, h in zip(shares, halves)], 0)
    came = swap(out, "mem", distance)
    kept = jnp.concatenate([share[:h] for share, h in zip(shares, halves)], 0) + came
    return cut(kept, halves)


def cut(value, sizes):
    ends = [sum(sizes[:i]) for i in range(len(sizes) + 1)]
    return [value[i:j] for i, j in zip(ends, ends[1:])]


def local(amplitudes, integrals, irrep_ef, irrep_ab):
    members = lax.axis_size("mem")
    groups = lax.axis_size("grp")
    me = lax.axis_index("mem")
    group = jnp.reshape(lax.axis_index("grp"), (1,)).astype(jnp.int32)
    rows, pairs = amplitudes.shape[0], integrals.shape[0]
    half, quarter = members // 2, members // 4
    allowed = irrep_ef[:, None] == irrep_ab[None, :]
    values = jnp.where(allowed, integrals, jnp.zeros_like(integrals))
    values = pltpu.with_memory_space_constraint(values, pltpu.VMEM)

    def blocked(pieces, blocks):
        if any(piece.shape[0] % 8 for piece in pieces):
            pieces = [jnp.concatenate(pieces, 0)]
        return product(pieces, values, group, groups, tuple(blocks))

    sizes = row_chunks(rows)
    far_ranges = [(sum(sizes[:c]), size) for c, size in enumerate(sizes)]
    source = amplitudes

    def piece(span, distance):
        return lax.dynamic_slice(source, (span[0], (me ^ distance) * pairs), (span[1], pairs))

    leads = [members - 1, members - 2]
    source, *leading = lax.optimization_barrier((source, *[piece(far_ranges[0], d) for d in leads]))
    leading = dict(zip(leads, leading))
    far = []
    for c, span in enumerate(far_ranges):
        outs = {d: piece(span, d) for d in range(half, members)}
        if c == 0:
            outs.update(leading)
        far.append({d: swap(out, "mem", d) for d, out in outs.items()})
    near = {d: piece((0, rows), d) for d in range(half)}
    near = {d: swap(out, "mem", d) if d else out for d, out in near.items()}

    order = reversed_bits(half)
    batches = [[[got[half + d] for d in order]] for got in far[:-1]] or [[]]
    batches[-1].append([near[d] for d in order])
    every = []
    for parts in batches:
        kept = columns_to_owner(sum(parts, []), blocked, groups)
        shares = cut(kept, [sum(p.shape[0] for p in part) for part in parts])
        if half > 1:
            shares = fold(shares, 1)
        every += shares
    bit = 2
    while bit < half:
        every = fold(every, bit)
        bit *= 2
    far_shares, near_share = every[:-1], every[-1]
    across = []
    if far_shares:
        across.append(swap(jnp.concatenate(far_shares, 0), "mem", half))
    folded = reversed_bits(quarter)
    ends = [far[-1][half + quarter + d] for d in folded]
    share = columns_to_owner(ends, blocked, groups)
    bit = 1
    while bit < quarter:
        [share] = fold([share], bit)
        bit *= 2
    joined = swap(share, "mem", quarter)
    share = columns_to_owner([far[-1][half + d] for d in range(quarter)], blocked, groups)
    blocks = cut(share, [sizes[-1]] * quarter)
    blocks[0] = blocks[0] + joined
    total = None
    for d in range(quarter - 1, -1, -1):
        came = swap(blocks[d], "mem", half + d)
        total = came if total is None else total + came
    return near_share + jnp.concatenate(across + [total], 0)


def solution(mesh):
    placed = (P("mem", "grp"), P(("grp", "mem"), None), P(("grp", "mem")), P())
    return jax.shard_map(
        local, mesh=mesh, in_specs=placed, out_specs=P("mem", "grp"), check_vma=False
    )
```

time: 271 us -> 222 us (0.82)
  blocking collectives: 145 us -> 0 us
  starting transfers between devices: 0.04 us -> 79.9 us
  matrix products: 17.7 us -> 0 us
  other arithmetic: 0 us -> 16.7 us
  Pallas kernels: 0 us -> 15.1 us
  between operations: 13.4 us -> 0.42 us
  local copies, waits for them, and re-layouts: 8.38 us -> 20.7 us
    all_to_all x1 -> x0, blocking collectives: 145 us -> none  [local(): lax.all_to_all(shaped, 'mem', split_axis=1, concat_axis=0, tiled=True)]
    ppermute x0 -> x31, waiting for transfers between devices: none -> 88.7 us  [swap(): return lax.ppermute(value, axis, [(i, i ^ distance) for i in range(count)])]
    ppermute x0 -> x31, starting transfers between devices: none -> 79.9 us  [swap(): return lax.ppermute(value, axis, [(i, i ^ distance) for i in range(count)])]
    unnamed x3 -> x0, waiting for transfers between devices: 65.1 us -> none
    reduce_scatter x1 -> x0, waiting for transfers between devices: 21 us -> none  [local(): result = lax.psum_scatter(row_share, 'grp', scatter_dimension=1, tiled=True)]
    dot_general x1 -> x0, matrix products: 17.7 us -> none  [local(): jnp.dot(arrived.reshape(-1, pair_cols), blocked, preferred_element_type=j...]
    select_n x0 -> x1, other arithmetic: none -> 15.1 us  [local(): values = jnp.where(allowed, integrals, jnp.zeros_like(integrals))]
    pallas_call x0 -> x12, Pallas kernels: none -> 15.1 us  [product(): pl.pallas_call(functools.partial(product_kernel, blocks), in_specs=[pl.Bl...]
  transfers between devices with their start and end apart: 2 -> 31, of which waited for: 2 -> 14; matrix products, arithmetic and copies ran while one was open for 0% -> 10% of each run, Pallas kernels for 0% -> 6%
where the time goes in v3:
time: 222 us; the launch traced here: 221 us
  waiting for transfers between devices  88.7 us (40%)
  starting transfers between devices  79.9 us (36%)
  local copies, waits for them, and re-layouts  20.7 us (9%)
  other arithmetic  16.7 us (8%)
  Pallas kernels  15.1 us (7%)
    ppermute x31, waiting for transfers between devices, swap(): return lax.ppermute(value, axis, [(i, i ^ distance) for i in range(count)])  88.7 us
    ppermute x31, starting transfers between devices, swap(): return lax.ppermute(value, axis, [(i, i ^ distance) for i in range(count)])  79.9 us
    select_n x1, other arithmetic, local(): values = jnp.where(allowed, integrals, jnp.zeros_like(integrals))  15.1 us
    pallas_call x12, Pallas kernels, product(): pl.pallas_call(functools.partial(product_kernel, blocks), in_specs=[pl.Bl...  15.1 us
    unnamed x22, local copies, waits for them, and re-layouts  11.6 us
    dynamic_slice x5, local copies, waits for them, and re-layouts, piece(): lax.dynamic_slice(source, (span[0], (me ^ distance) * pairs), (span[1], p...  8.48 us
  transfers between devices with their start and end apart: 31, of which 14 were waited for; matrix products, arithmetic and copies ran while one was open for 10% of the time, Pallas kernels for 6%

profile of v3, /device:TPU:0, one launch (start us, length us, event | category | flops | bytes accessed | tf_op | source)
XLA Modules:
  0.0 221.4 jit_solution(6195032844987509337)
XLA Ops:
  0.0 1.0 constant_dynamic-slice_fusion.6
  1.0 1.0 constant_dynamic-slice_fusion.4
  2.0 4.1 %collective-permute-start = (bf16[8,8192]{1,0:T(8,128)(2,1)S(1)}, bf16[8,8192]{1,0:T(8,128)(2,1)S(1)}, u32[]{:S(2)}, u32[]{:S(2)}) collective-permute-start(bf16[8,8192]{1,0:T(8,128)(2,1)S(1)} %get-tuple-element.16), channel_id=1, source_target_pairs={{0,4},{1,5},{2,6},{3,7},{4,0},{5,1},{6,2},{7,3},{8,12},{9,13},{10,... | collective-permute-start | bytes 393224 | tf_op jit(solution)/shard_map/ppermute | solution.py:16
  6.1 1.3 collective-permute-start.2
  7.4 3.6 %collective-permute-start.1 = (bf16[8,8192]{1,0:T(8,128)(2,1)S(1)}, bf16[8,8192]{1,0:T(8,128)(2,1)S(1)}, u32[]{:S(2)}, u32[]{:S(2)}) collective-permute-start(bf16[8,8192]{1,0:T(8,128)(2,1)S(1)} %get-tuple-element.9), channel_id=1, source_target_pairs={{0,6},{1,7},{2,4},{3,5},{4,2},{5,3},{6,0},{7,1},{8,14},{9,15},{10,... | collective-permute-start | bytes 393224 | tf_op jit(solution)/shard_map/ppermute | solution.py:16
  11.0 15.1 %compare_select_fusion.refs_4_.refs_8_.refs_2_ = bf16[8192,1024]{1,0:T(8,128)(2,1)} fusion(bf16[8192,1024]{1,0:T(8,128)(2,1)} %param.5, s32[1024]{0:T(1024)} %param.7, s32[8192]{0:T(1024)} %param.6), kind=kLoop, calls=%fused_computation | loop fusion | flops 16777216 | bytes 33591296 | tf_op jit(solution)/shard_map/jit(_where)/select_n | solution.py:108
  26.2 5.8 %copy-done = bf16[8192,1024]{1,0:T(8,128)(2,1)S(1)} copy-done((bf16[8192,1024]{1,0:T(8,128)(2,1)S(1)}, bf16[8192,1024]{1,0:T(8,128)(2,1)}, u32[]{:S(2)}) %copy-start) | copy-done | bytes 16777240
  31.9 1.6 shard_map.47
  34.8 1.6 collective-permute-start.5
  36.5 2.5 %constant_dynamic-slice_fusion.8 = (bf16[24,8192]{1,0:T(8,128)(2,1)S(1)}, bf16[24,8192]{1,0:T(8,128)(2,1)}, bf16[24,8192]{1,0:T(8,128)(2,1)S(1)}, bf16[24,8192]{1,0:T(8,128)(2,1)S(1)}) fusion(bf16[48,65536]{1,0:T(8,128)(2,1)} %param.4, s32[]{:T(128)S(6)} %select_n.36, s32[]{:T(128)S(6)} %select_n.37, s32[]{:T(128)S(6)} %select_n.39, s32[]{:T(128)S(6)} %select_n.38), kind=kLoop, calls=%fused_computation.29 | loop fusion | bytes 3145744 | tf_op jit(solution)/shard_map/dynamic_slice | solution.py:121
  39.0 6.7 %collective-permute-start.19 = (bf16[24,8192]{1,0:T(8,128)(2,1)S(1)}, bf16[24,8192]{1,0:T(8,128)(2,1)S(1)}, u32[]{:S(2)}, u32[]{:S(2)}) collective-permute-start(bf16[24,8192]{1,0:T(8,128)(2,1)S(1)} %get-tuple-element.14), channel_id=1, source_target_pairs={{0,4},{1,5},{2,6},{3,7},{4,0},{5,1},{6,2},{7,3},{8,12},{9,13},{10,... | collective-permute-start | bytes 1179656 | tf_op jit(solution)/shard_map/ppermute | solution.py:16
  45.7 0.9 collective-permute-start.24
  46.6 3.8 %collective-permute-start.25 = (bf16[24,8192]{1,0:T(8,128)(2,1)S(1)}, bf16[24,8192]{1,0:T(8,128)(2,1)S(1)}, u32[]{:S(2)}, u32[]{:S(2)}) collective-permute-start(bf16[24,8192]{1,0:T(8,128)(2,1)S(1)} %get-tuple-element.11), channel_id=1, source_target_pairs={{0,7},{1,6},{2,5},{3,4},{4,3},{5,2},{6,1},{7,0},{8,15},{9,14},{10,... | collective-permute-start | bytes 1179656 | tf_op jit(solution)/shard_map/ppermute | solution.py:16
  50.4 0.9 shard_map.46
  52.5 2.0 constant_dynamic-slice_fusion.12
  54.5 1.4 collective-permute-done.6
  55.9 0.9 collective-permute-start.10
  56.8 2.0 constant_dynamic-slice_fusion
  58.9 27.3 %collective-permute-done.10.refs_3_ = bf16[16,8192]{1,0:T(8,128)(2,1)S(1)} collective-permute-done((bf16[16,8192]{1,0:T(8,128)(2,1)}, bf16[16,8192]{1,0:T(8,128)(2,1)S(1)}, u32[]{:S(2)}, u32[]{:S(2)}) %collective-permute-start.10) | collective-permute-done | bytes 262176 | tf_op jit(solution)/shard_map/ppermute | solution.py:16
  86.1 39.6 %collective-permute-start.11 = (bf16[48,8192]{1,0:T(8,128)(2,1)S(1)}, bf16[48,8192]{1,0:T(8,128)(2,1)S(1)}, u32[]{:S(2)}, u32[]{:S(2)}) collective-permute-start(bf16[48,8192]{1,0:T(8,128)(2,1)S(1)} %get-tuple-element.19), channel_id=1, source_target_pairs={{0,2},{1,3},{2,0},{3,1},{4,6},{5,7},{6,4},{7,5},{8,10},{9,11},{10,... | collective-permute-start | bytes 2359304 | tf_op jit(solution)/shard_map/ppermute | solution.py:16
  125.7 1.0 collective-permute-start.12
  127.9 5.8 %copy-done.1 = bf16[8192,1024]{1,0:T(8,128)(2,1)S(1)} copy-done((bf16[8192,1024]{1,0:T(8,128)(2,1)S(1)}, bf16[8192,1024]{1,0:T(8,128)(2,1)}, u32[]{:S(2)}) %copy-start.1) | copy-done | bytes 16777240
  133.7 1.6 shard_map.56
  135.3 1.1 collective-permute-start.7
  136.4 0.9 shard_map.54
  137.3 0.9 shard_map.52
  138.2 0.9 shard_map.57
  139.2 0.9 shard_map.55
  140.1 25.5 %collective-permute-done.7.refs_0_ = bf16[16,8192]{1,0:T(8,128)(2,1)S(1)} collective-permute-done((bf16[16,8192]{1,0:T(8,128)(2,1)S(1)}, bf16[16,8192]{1,0:T(8,128)(2,1)S(1)}, u32[]{:S(2)}, u32[]{:S(2)}) %collective-permute-start.7) | collective-permute-done | bytes 262176 | tf_op jit(solution)/shard_map/ppermute | solution.py:16
  165.6 3.9 %collective-permute-start.9 = (bf16[16,8192]{1,0:T(8,128)(2,1)S(1)}, bf16[16,8192]{1,0:T(8,128)(2,1)S(1)}, u32[]{:S(2)}, u32[]{:S(2)}) collective-permute-start(bf16[16,8192]{1,0:T(8,128)(2,1)S(1)} %get-tuple-element.22), channel_id=1, source_target_pairs={{0,5},{1,4},{2,7},{3,6},{4,1},{5,0},{6,3},{7,2},{8,13},{9,12},{10,... | collective-permute-start | bytes 786440 | tf_op jit(solution)/shard_map/ppermute | solution.py:16
  169.5 1.6 shard_map.53
  171.2 5.3 %collective-permute-done.8.refs_1_ = bf16[16,8192]{1,0:T(8,128)(2,1)S(1)} collective-permute-done((bf16[16,8192]{1,0:T(8,128)(2,1)S(1)}, bf16[16,8192]{1,0:T(8,128)(2,1)S(1)}, u32[]{:S(2)}, u32[]{:S(2)}) %collective-permute-start.8) | collective-permute-done | bytes 262176 | tf_op jit(solution)/shard_map/ppermute | solution.py:16
  176.5 15.1 %collective-permute-done.9.refs_2_ = bf16[16,8192]{1,0:T(8,128)(2,1)S(1)} collective-permute-done((bf16[16,8192]{1,0:T(8,128)(2,1)S(1)}, bf16[16,8192]{1,0:T(8,128)(2,1)S(1)}, u32[]{:S(2)}, u32[]{:S(2)}) %collective-permute-start.9) | collective-permute-done | bytes 262176 | tf_op jit(solution)/shard_map/ppermute | solution.py:16
  191.6 1.2 collective-permute-start.27
  192.8 2.4 %shard_map.50 = f32[512,256]{1,0:T(8,128)S(1)} custom-call(s32[1]{0:T(128)} %bitcast.group, bf16[16,8192]{1,0:T(8,128)(2,1)S(1)} %collective-permute-done.7.refs_0_, bf16[16,8192]{1,0:T(8,128)(2,1)S(1)} %collective-permute-done.8.refs_1_, bf16[16,8192]{1,0:T(8,128)(2,1)S(1)} %collective-permute-done.9.refs_2_, ...), custom_call_target="tpu_custom_call" | custom-call | flops 2147483648 | bytes 8388608 | tf_op jit(solution)/shard_map/pallas_call | solution.py:52
  195.3 0.9 collective-permute-start.22
  196.8 1.3 shard_map.51
  198.2 0.9 collective-permute-start.15
  199.5 1.3 shard_map.49
  200.8 5.5 %collective-permute-done.15 = f32[256,256]{1,0:T(8,128)S(1)} collective-permute-done((f32[256,256]{1,0:T(8,128)S(1)}, f32[256,256]{1,0:T(8,128)S(1)}, u32[]{:S(2)}, u32[]{:S(2)}) %collective-permute-start.15) | collective-permute-done | bytes 262176 | tf_op jit(solution)/shard_map/ppermute | solution.py:16
  206.5 1.6 collective-permute-start.16
  208.1 3.4 %collective-permute-done.16 = f32[128,256]{1,0:T(8,128)S(1)} collective-permute-done((f32[128,256]{1,0:T(8,128)S(1)}, f32[128,256]{1,0:T(8,128)S(1)}, u32[]{:S(2)}, u32[]{:S(2)}) %collective-permute-start.16) | collective-permute-done | bytes 131104 | tf_op jit(solution)/shard_map/ppermute | solution.py:16
  212.0 2.1 collective-permute-start.23
  214.1 1.5 collective-permute-start.30
  216.0 1.1 collective-permute-start.18
  217.1 0.9 collective-permute-done.23
  218.0 1.3 collective-permute-done.30
  219.3 1.5 collective-permute-done.18
  (81 shorter events, 6.5 us)
Async XLA Ops:
  2.0 24.1 %collective-permute-start = (bf16[8,8192]{1,0:T(8,128)(2,1)S(1)}, bf16[8,8192]{1,0:T(8,128)(2,1)S(1)}, u32[]{:S(2)}, u32[]{:S(2)}) collective-permute-start(bf16[8,8192]{1,0:T(8,128)(2,1)S(1)} %get-tuple-element.16), channel_id=1, source_target_pairs={{0,4},{1,5},{2,6},{3,7},{4,0},{5,1},{6,2},{7,3},{8,12},{9,13},{10,... | collective-permute-start | bytes 393224 | tf_op jit(solution)/shard_map/ppermute | solution.py:16
  6.1 20.0 %collective-permute-start.2 = (bf16[8,8192]{1,0:T(8,128)(2,1)S(1)}, bf16[8,8192]{1,0:T(8,128)(2,1)S(1)}, u32[]{:S(2)}, u32[]{:S(2)}) collective-permute-start(bf16[8,8192]{1,0:T(8,128)(2,1)S(1)} %get-tuple-element.15), channel_id=1, source_target_pairs={{0,5},{1,4},{2,7},{3,6},{4,1},{5,0},{6,3},{7,2},{8,13},{9,12},{10,... | collective-permute-start | bytes 393224 | tf_op jit(solution)/shard_map/ppermute | solution.py:16
  7.4 18.7 %collective-permute-start.1 = (bf16[8,8192]{1,0:T(8,128)(2,1)S(1)}, bf16[8,8192]{1,0:T(8,128)(2,1)S(1)}, u32[]{:S(2)}, u32[]{:S(2)}) collective-permute-start(bf16[8,8192]{1,0:T(8,128)(2,1)S(1)} %get-tuple-element.9), channel_id=1, source_target_pairs={{0,6},{1,7},{2,4},{3,5},{4,2},{5,3},{6,0},{7,1},{8,14},{9,15},{10,... | collective-permute-start | bytes 393224 | tf_op jit(solution)/shard_map/ppermute | solution.py:16
  11.0 15.1 %collective-permute-start.3 = (bf16[8,8192]{1,0:T(8,128)(2,1)S(1)}, bf16[8,8192]{1,0:T(8,128)(2,1)S(1)}, u32[]{:S(2)}, u32[]{:S(2)}) collective-permute-start(bf16[8,8192]{1,0:T(8,128)(2,1)S(1)} %get-tuple-element.10), channel_id=1, source_target_pairs={{0,7},{1,6},{2,5},{3,4},{4,3},{5,2},{6,1},{7,0},{8,15},{9,14},{10,... | collective-permute-start | bytes 393224 | tf_op jit(solution)/shard_map/ppermute | solution.py:16
  26.2 5.8 %copy-start = (bf16[8192,1024]{1,0:T(8,128)(2,1)S(1)}, bf16[8192,1024]{1,0:T(8,128)(2,1)}, u32[]{:S(2)}) copy-start(bf16[8192,1024]{1,0:T(8,128)(2,1)} %compare_select_fusion.refs_4_.refs_8_.refs_2_) | copy-start | bytes 50331652
  31.9 18.5 %slice-start = ((s8[16777216]{0:T(1024)(128)(4,1)}), s8[4194304]{0:T(1024)(128)(4,1)S(1)}, s32[]{:S(2)}) async-start(s8[16777216]{0:T(1024)(128)(4,1)} %bitcast.1), calls=%async_computation | async-start | bytes 8388608
  31.9 18.5 %slice-start.1 = ((s8[16777216]{0:T(1024)(128)(4,1)}), s8[4194304]{0:T(1024)(128)(4,1)S(1)}, s32[]{:S(2)}) async-start(s8[16777216]{0:T(1024)(128)(4,1)} %bitcast.1), calls=%async_computation.1 | async-start | bytes 8388608
  33.5 16.9 %slice-start.2 = ((s8[16777216]{0:T(1024)(128)(4,1)}), s8[4194304]{0:T(1024)(128)(4,1)S(1)}, s32[]{:S(2)}) async-start(s8[16777216]{0:T(1024)(128)(4,1)} %bitcast.1), calls=%async_computation.2 | async-start | bytes 8388608
  33.5 16.9 %slice-start.3 = ((s8[16777216]{0:T(1024)(128)(4,1)}), s8[4194304]{0:T(1024)(128)(4,1)S(1)}, s32[]{:S(2)}) async-start(s8[16777216]{0:T(1024)(128)(4,1)} %bitcast.1), calls=%async_computation.3 | async-start | bytes 8388608
  33.5 1.3 collective-permute-start.4
  34.8 16.5 %collective-permute-start.5 = (f32[32,256]{1,0:T(8,128)S(1)}, f32[32,256]{1,0:T(8,128)S(1)}, u32[]{:S(2)}, u32[]{:S(2)}) collective-permute-start(f32[32,256]{1,0:T(8,128)S(1)} %slice_add_fusion.7), channel_id=1, source_target_pairs={{0,16},{8,24},{16,0},{24,8},{1,17},{9,25},{17,1},{25,9},{2,18},{10... | collective-permute-start | bytes 98312 | tf_op jit(solution)/shard_map/ppermute | solution.py:16
  39.0 96.3 %collective-permute-start.19 = (bf16[24,8192]{1,0:T(8,128)(2,1)S(1)}, bf16[24,8192]{1,0:T(8,128)(2,1)S(1)}, u32[]{:S(2)}, u32[]{:S(2)}) collective-permute-start(bf16[24,8192]{1,0:T(8,128)(2,1)S(1)} %get-tuple-element.14), channel_id=1, source_target_pairs={{0,4},{1,5},{2,6},{3,7},{4,0},{5,1},{6,2},{7,3},{8,12},{9,13},{10,... | collective-permute-start | bytes 1179656 | tf_op jit(solution)/shard_map/ppermute | solution.py:16
  45.7 90.7 %collective-permute-start.20 = (bf16[24,8192]{1,0:T(8,128)(2,1)S(1)}, bf16[24,8192]{1,0:T(8,128)(2,1)S(1)}, u32[]{:S(2)}, u32[]{:S(2)}) collective-permute-start(bf16[24,8192]{1,0:T(8,128)(2,1)S(1)} %get-tuple-element.13), channel_id=1, source_target_pairs={{0,5},{1,4},{2,7},{3,6},{4,1},{5,0},{6,3},{7,2},{8,13},{9,12},{10,... | collective-permute-start | bytes 1179656 | tf_op jit(solution)/shard_map/ppermute | solution.py:16
  45.7 80.0 %collective-permute-start.24 = (bf16[24,8192]{1,0:T(8,128)(2,1)}, bf16[24,8192]{1,0:T(8,128)(2,1)S(1)}, u32[]{:S(2)}, u32[]{:S(2)}) collective-permute-start(bf16[24,8192]{1,0:T(8,128)(2,1)} %get-tuple-element.12), channel_id=1, source_target_pairs={{0,6},{1,7},{2,4},{3,5},{4,2},{5,3},{6,0},{7,1},{8,14},{9,15},{10,... | collective-permute-start | bytes 1179656 | tf_op jit(solution)/shard_map/ppermute | solution.py:16
  46.6 80.1 %collective-permute-start.25 = (bf16[24,8192]{1,0:T(8,128)(2,1)S(1)}, bf16[24,8192]{1,0:T(8,128)(2,1)S(1)}, u32[]{:S(2)}, u32[]{:S(2)}) collective-permute-start(bf16[24,8192]{1,0:T(8,128)(2,1)S(1)} %get-tuple-element.11), channel_id=1, source_target_pairs={{0,7},{1,6},{2,5},{3,4},{4,3},{5,2},{6,1},{7,0},{8,15},{9,14},{10,... | collective-permute-start | bytes 1179656 | tf_op jit(solution)/shard_map/ppermute | solution.py:16
  51.3 0.6 copy-start.2
  52.0 3.9 %collective-permute-start.6 = (f32[16,256]{1,0:T(8,128)}, f32[16,256]{1,0:T(8,128)S(1)}, u32[]{:S(2)}, u32[]{:S(2)}) collective-permute-start(f32[16,256]{1,0:T(8,128)} %slice.118), channel_id=1, source_target_pairs={{0,1},{1,0},{2,3},{3,2},{4,5},{5,4},{6,7},{7,6},{8,9},{9,8},{10,11... | collective-permute-start | bytes 49160 | tf_op jit(solution)/shard_map/ppermute | solution.py:16
  55.9 30.2 %collective-permute-start.10 = (bf16[16,8192]{1,0:T(8,128)(2,1)}, bf16[16,8192]{1,0:T(8,128)(2,1)S(1)}, u32[]{:S(2)}, u32[]{:S(2)}) collective-permute-start(bf16[16,8192]{1,0:T(8,128)(2,1)} %get-tuple-element.21), channel_id=1, source_target_pairs={{0,7},{1,6},{2,5},{3,4},{4,3},{5,2},{6,1},{7,0},{8,15},{9,14},{10,... | collective-permute-start | bytes 786440 | tf_op jit(solution)/shard_map/ppermute | solution.py:16
  86.1 106.6 %collective-permute-start.11 = (bf16[48,8192]{1,0:T(8,128)(2,1)S(1)}, bf16[48,8192]{1,0:T(8,128)(2,1)S(1)}, u32[]{:S(2)}, u32[]{:S(2)}) collective-permute-start(bf16[48,8192]{1,0:T(8,128)(2,1)S(1)} %get-tuple-element.19), channel_id=1, source_target_pairs={{0,2},{1,3},{2,0},{3,1},{4,6},{5,7},{6,4},{7,5},{8,10},{9,11},{10,... | collective-permute-start | bytes 2359304 | tf_op jit(solution)/shard_map/ppermute | solution.py:16
  125.7 67.0 %collective-permute-start.12 = (bf16[48,8192]{1,0:T(8,128)(2,1)S(1)}, bf16[48,8192]{1,0:T(8,128)(2,1)S(1)}, u32[]{:S(2)}, u32[]{:S(2)}) collective-permute-start(bf16[48,8192]{1,0:T(8,128)(2,1)S(1)} %get-tuple-element.18), channel_id=1, source_target_pairs={{0,1},{1,0},{2,3},{3,2},{4,5},{5,4},{6,7},{7,6},{8,9},{9,8},{10,11... | collective-permute-start | bytes 2359304 | tf_op jit(solution)/shard_map/ppermute | solution.py:16
  126.7 66.0 %collective-permute-start.13 = (bf16[48,8192]{1,0:T(8,128)(2,1)S(1)}, bf16[48,8192]{1,0:T(8,128)(2,1)S(1)}, u32[]{:S(2)}, u32[]{:S(2)}) collective-permute-start(bf16[48,8192]{1,0:T(8,128)(2,1)S(1)} %get-tuple-element.17), channel_id=1, source_target_pairs={{0,3},{1,2},{2,1},{3,0},{4,7},{5,6},{6,5},{7,4},{8,11},{9,10},{10,... | collective-permute-start | bytes 2359304 | tf_op jit(solution)/shard_map/ppermute | solution.py:16
  127.9 5.8 %copy-start.1 = (bf16[8192,1024]{1,0:T(8,128)(2,1)S(1)}, bf16[8192,1024]{1,0:T(8,128)(2,1)}, u32[]{:S(2)}) copy-start(bf16[8192,1024]{1,0:T(8,128)(2,1)} %compare_select_fusion.refs_4_.refs_8_.refs_2_) | copy-start | bytes 50331652
  135.3 30.3 %collective-permute-start.7 = (bf16[16,8192]{1,0:T(8,128)(2,1)S(1)}, bf16[16,8192]{1,0:T(8,128)(2,1)S(1)}, u32[]{:S(2)}, u32[]{:S(2)}) collective-permute-start(bf16[16,8192]{1,0:T(8,128)(2,1)S(1)} %get-tuple-element.24), channel_id=1, source_target_pairs={{0,4},{1,5},{2,6},{3,7},{4,0},{5,1},{6,2},{7,3},{8,12},{9,13},{10,... | collective-permute-start | bytes 786440 | tf_op jit(solution)/shard_map/ppermute | solution.py:16
  136.4 29.2 %collective-permute-start.26 = (f32[96,256]{1,0:T(8,128)S(1)}, f32[96,256]{1,0:T(8,128)S(1)}, u32[]{:S(2)}, u32[]{:S(2)}) collective-permute-start(f32[96,256]{1,0:T(8,128)S(1)} %shard_map.56), channel_id=1, source_target_pairs={{0,8},{8,0},{16,24},{24,16},{1,9},{9,1},{17,25},{25,17},{2,10},{10... | collective-permute-start | bytes 294920 | tf_op jit(solution)/shard_map/ppermute | solution.py:16
  139.1 53.6 %slice-start.4 = ((s8[16777216]{0:T(1024)(128)(4,1)}), s8[4194304]{0:T(1024)(128)(4,1)S(1)}, s32[]{:S(2)}) async-start(s8[16777216]{0:T(1024)(128)(4,1)} %bitcast.3), calls=%async_computation.4 | async-start | bytes 8388608
  139.2 53.6 %slice-start.5 = ((s8[16777216]{0:T(1024)(128)(4,1)}), s8[4194304]{0:T(1024)(128)(4,1)S(1)}, s32[]{:S(2)}) async-start(s8[16777216]{0:T(1024)(128)(4,1)} %bitcast.3), calls=%async_computation.5 | async-start | bytes 8388608
  165.6 10.9 %collective-permute-start.8 = (bf16[16,8192]{1,0:T(8,128)(2,1)S(1)}, bf16[16,8192]{1,0:T(8,128)(2,1)S(1)}, u32[]{:S(2)}, u32[]{:S(2)}) collective-permute-start(bf16[16,8192]{1,0:T(8,128)(2,1)S(1)} %get-tuple-element.23), channel_id=1, source_target_pairs={{0,6},{1,7},{2,4},{3,5},{4,2},{5,3},{6,0},{7,1},{8,14},{9,15},{10,... | collective-permute-start | bytes 786440 | tf_op jit(solution)/shard_map/ppermute | solution.py:16
  165.6 27.2 %slice-start.6 = ((s8[16777216]{0:T(1024)(128)(4,1)}), s8[4194304]{0:T(1024)(128)(4,1)S(1)}, s32[]{:S(2)}) async-start(s8[16777216]{0:T(1024)(128)(4,1)} %bitcast.3), calls=%async_computation.6 | async-start | bytes 8388608
  165.6 27.2 %slice-start.7 = ((s8[16777216]{0:T(1024)(128)(4,1)}), s8[4194304]{0:T(1024)(128)(4,1)S(1)}, s32[]{:S(2)}) async-start(s8[16777216]{0:T(1024)(128)(4,1)} %bitcast.3), calls=%async_computation.7 | async-start | bytes 8388608
  165.6 25.9 %collective-permute-start.9 = (bf16[16,8192]{1,0:T(8,128)(2,1)S(1)}, bf16[16,8192]{1,0:T(8,128)(2,1)S(1)}, u32[]{:S(2)}, u32[]{:S(2)}) collective-permute-start(bf16[16,8192]{1,0:T(8,128)(2,1)S(1)} %get-tuple-element.22), channel_id=1, source_target_pairs={{0,5},{1,4},{2,7},{3,6},{4,1},{5,0},{6,3},{7,2},{8,13},{9,12},{10,... | collective-permute-start | bytes 786440 | tf_op jit(solution)/shard_map/ppermute | solution.py:16
  176.5 18.8 %collective-permute-start.21 = (f32[96,256]{1,0:T(8,128)S(1)}, f32[96,256]{1,0:T(8,128)S(1)}, u32[]{:S(2)}, u32[]{:S(2)}) collective-permute-start(f32[96,256]{1,0:T(8,128)S(1)} %shard_map.53), channel_id=1, source_target_pairs={{0,8},{8,0},{16,24},{24,16},{1,9},{9,1},{17,25},{25,17},{2,10},{10... | collective-permute-start | bytes 294920 | tf_op jit(solution)/shard_map/ppermute | solution.py:16
  191.6 4.7 %collective-permute-start.27 = (f32[48,256]{1,0:T(8,128)S(1)}, f32[48,256]{1,0:T(8,128)S(1)}, u32[]{:S(2)}, u32[]{:S(2)}) collective-permute-start(f32[48,256]{1,0:T(8,128)S(1)} %slice_add_fusion.2), channel_id=1, source_target_pairs={{0,16},{8,24},{16,0},{24,8},{1,17},{9,25},{17,1},{25,9},{2,18},{10... | collective-permute-start | bytes 147464 | tf_op jit(solution)/shard_map/ppermute | solution.py:16
  195.2 2.9 %collective-permute-start.14 = (f32[512,256]{1,0:T(8,128)S(1)}, f32[512,256]{1,0:T(8,128)S(1)}, u32[]{:S(2)}, u32[]{:S(2)}) collective-permute-start(f32[512,256]{1,0:T(8,128)S(1)} %shard_map.50), channel_id=1, source_target_pairs={{0,8},{8,0},{16,24},{24,16},{1,9},{9,1},{17,25},{25,17},{2,10},{10... | collective-permute-start | bytes 1572872 | tf_op jit(solution)/shard_map/ppermute | solution.py:16
  195.3 4.2 %collective-permute-start.22 = (f32[48,256]{1,0:T(8,128)S(1)}, f32[48,256]{1,0:T(8,128)S(1)}, u32[]{:S(2)}, u32[]{:S(2)}) collective-permute-start(f32[48,256]{1,0:T(8,128)S(1)} %slice_add_fusion.4), channel_id=1, source_target_pairs={{0,16},{8,24},{16,0},{24,8},{1,17},{9,25},{17,1},{25,9},{2,18},{10... | collective-permute-start | bytes 147464 | tf_op jit(solution)/shard_map/ppermute | solution.py:16
  196.2 11.8 %collective-permute-start.28 = (f32[24,256]{1,0:T(8,128)S(1)}, f32[24,256]{1,0:T(8,128)S(1)}, u32[]{:S(2)}, u32[]{:S(2)}) collective-permute-start(f32[24,256]{1,0:T(8,128)S(1)} %slice.139), channel_id=1, source_target_pairs={{0,1},{1,0},{2,3},{3,2},{4,5},{5,4},{6,7},{7,6},{8,9},{9,8},{10,11... | collective-permute-start | bytes 73736 | tf_op jit(solution)/shard_map/ppermute | solution.py:16
  198.2 8.2 %collective-permute-start.15 = (f32[256,256]{1,0:T(8,128)S(1)}, f32[256,256]{1,0:T(8,128)S(1)}, u32[]{:S(2)}, u32[]{:S(2)}) collective-permute-start(f32[256,256]{1,0:T(8,128)S(1)} %slice_add_fusion), channel_id=1, source_target_pairs={{0,16},{8,24},{16,0},{24,8},{1,17},{9,25},{17,1},{25,9},{2,18},{10... | collective-permute-start | bytes 786440 | tf_op jit(solution)/shard_map/ppermute | solution.py:16
  206.5 5.0 %collective-permute-start.16 = (f32[128,256]{1,0:T(8,128)S(1)}, f32[128,256]{1,0:T(8,128)S(1)}, u32[]{:S(2)}, u32[]{:S(2)}) collective-permute-start(f32[128,256]{1,0:T(8,128)S(1)} %pad_maximum_fusion), channel_id=1, source_target_pairs={{0,1},{1,0},{2,3},{3,2},{4,5},{5,4},{6,7},{7,6},{8,9},{9,8},{10,11... | collective-permute-start | bytes 393224 | tf_op jit(solution)/shard_map/ppermute | solution.py:16
  208.1 3.9 %collective-permute-start.29 = (f32[24,256]{1,0:T(8,128)S(1)}, f32[24,256]{1,0:T(8,128)S(1)}, u32[]{:S(2)}, u32[]{:S(2)}) collective-permute-start(f32[24,256]{1,0:T(8,128)S(1)} %slice_add_fusion.9), channel_id=1, source_target_pairs={{0,2},{1,3},{2,0},{3,1},{4,6},{5,7},{6,4},{7,5},{8,10},{9,11},{10,... | collective-permute-start | bytes 73736 | tf_op jit(solution)/shard_map/ppermute | solution.py:16
  211.6 4.4 %collective-permute-start.17 = (f32[72,256]{1,0:T(8,128)S(1)}, f32[72,256]{1,0:T(8,128)S(1)}, u32[]{:S(2)}, u32[]{:S(2)}) collective-permute-start(f32[72,256]{1,0:T(8,128)S(1)} %pad_maximum_fusion.1), channel_id=1, source_target_pairs={{0,2},{1,3},{2,0},{3,1},{4,6},{5,7},{6,4},{7,5},{8,10},{9,11},{10,... | collective-permute-start | bytes 221192 | tf_op jit(solution)/shard_map/ppermute | solution.py:16
  212.0 6.1 %collective-permute-start.23 = (f32[24,256]{1,0:T(8,128)S(1)}, f32[24,256]{1,0:T(8,128)S(1)}, u32[]{:S(2)}, u32[]{:S(2)}) collective-permute-start(f32[24,256]{1,0:T(8,128)S(1)} %get-tuple-element.36), channel_id=1, source_target_pairs={{0,5},{1,4},{2,7},{3,6},{4,1},{5,0},{6,3},{7,2},{8,13},{9,12},{10,... | collective-permute-start | bytes 73736 | tf_op jit(solution)/shard_map/ppermute | solution.py:16
  214.1 5.3 %collective-permute-start.30 = (f32[24,256]{1,0:T(8,128)S(1)}, f32[24,256]{1,0:T(8,128)S(1)}, u32[]{:S(2)}, u32[]{:S(2)}) collective-permute-start(f32[24,256]{1,0:T(8,128)S(1)} %get-tuple-element.35), channel_id=1, source_target_pairs={{0,4},{1,5},{2,6},{3,7},{4,0},{5,1},{6,2},{7,3},{8,12},{9,13},{10,... | collective-permute-start | bytes 73736 | tf_op jit(solution)/shard_map/ppermute | solution.py:16
  216.0 4.8 %collective-permute-start.18 = (f32[24,256]{1,0:T(8,128)S(1)}, f32[24,256]{1,0:T(8,128)S(1)}, u32[]{:S(2)}, u32[]{:S(2)}) collective-permute-start(f32[24,256]{1,0:T(8,128)S(1)} %concatenate.24), channel_id=1, source_target_pairs={{0,4},{1,5},{2,6},{3,7},{4,0},{5,1},{6,2},{7,3},{8,12},{9,13},{10,... | collective-permute-start | bytes 73736 | tf_op jit(solution)/shard_map/ppermute | solution.py:16

commit v4 on v3

--- a/solution.py
+++ b/solution.py
@@ -64,24 +64,15 @@
 
 
 def columns_to_owner(pieces, product_of, groups):
-    rows = sum(piece.shape[0] for piece in pieces)
-    came = {j: [] for j in range(groups)}
+    def total(j, count):
+        if count == 1:
+            return product_of(pieces, [j])
+        bit = count // 2
+        came = swap(total(j + bit, bit), "grp", bit)
+        own = total(j, bit)
+        return own + came
 
-    def term(blocks):
-        return product_of(pieces, blocks)
-
-    bit = 1
-    while bit < groups:
-        blocks = range(bit, groups, 2 * bit)
-        out = term(blocks)
-        if came[bit]:
-            out = out + sum(jnp.concatenate(parts, 0) for parts in zip(*[came[j] for j in blocks]))
-        got = cut(swap(out, "grp", bit), [rows] * len(blocks))
-        for j, part in zip(blocks, got):
-            came[j - bit].append(part)
-        bit *= 2
-    out = term([0])
-    return out + sum(came[0])
+    return total(0, groups)
 
 
 def fold(shares, distance):
@@ -162,7 +153,7 @@
     blocks = cut(share, [sizes[-1]] * quarter)
     blocks[0] = blocks[0] + joined
     total = None
-    for d in range(quarter - 1, -1, -1):
+    for d in range(quarter):
         came = swap(blocks[d], "mem", half + d)
         total = came if total is None else total + came
     return near_share + jnp.concatenate(across + [total], 0)

time: 222 us -> 213 us (0.959)
  starting transfers between devices: 79.9 us -> 72 us
    ppermute x31 -> x35, starting transfers between devices: 79.9 us -> 72 us  [swap(): return lax.ppermute(value, axis, [(i, i ^ distance) for i in range(count)])]
    pallas_call x12 -> x16, Pallas kernels: 15.1 us -> 15.9 us  [product(): pl.pallas_call(functools.partial(product_kernel, blocks), in_specs=[pl.Bl...]
    ppermute x31 -> x35, waiting for transfers between devices: 88.7 us -> 88.5 us  [swap(): return lax.ppermute(value, axis, [(i, i ^ distance) for i in range(count)])]
    unnamed x22 -> x20, local copies, waits for them, and re-layouts: 11.6 us -> 11.6 us
  transfers between devices with their start and end apart: 31 -> 35, of which waited for: 14 -> 11; matrix products, arithmetic and copies ran while one was open for 10% -> 10% of each run, Pallas kernels for 6% -> 7%
where the time goes in v4:
time: 213 us
  waiting for transfers between devices  88.5 us (42%)
  starting transfers between devices  72 us (34%)
  local copies, waits for them, and re-layouts  19.9 us (9%)
  other arithmetic  15.9 us (7%)
  Pallas kernels  15.9 us (7%)
    ppermute x35, waiting for transfers between devices, swap(): return lax.ppermute(value, axis, [(i, i ^ distance) for i in range(count)])  88.5 us
    ppermute x35, starting transfers between devices, swap(): return lax.ppermute(value, axis, [(i, i ^ distance) for i in range(count)])  72 us
    pallas_call x16, Pallas kernels, product(): pl.pallas_call(functools.partial(product_kernel, blocks), in_specs=[pl.Bl...  15.9 us
    select_n x1, other arithmetic, local(): values = jnp.where(allowed, integrals, jnp.zeros_like(integrals))  15.1 us
    unnamed x20, local copies, waits for them, and re-layouts  11.6 us
    dynamic_slice x5, local copies, waits for them, and re-layouts, piece(): lax.dynamic_slice(source, (span[0], (me ^ distance) * pairs), (span[1], p...  8.3 us
  transfers between devices with their start and end apart: 35, of which 11 were waited for; matrix products, arithmetic and copies ran while one was open for 10% of the time, Pallas kernels for 7%

profile of v4, /device:TPU:0, one launch (start us, length us, event | category | flops | bytes accessed | tf_op | source)
XLA Modules:
  0.0 212.8 jit_solution(4648295280743535506)
XLA Ops:
  0.0 1.0 constant_dynamic-slice_fusion.6
  1.0 1.0 constant_dynamic-slice_fusion.4
  2.0 4.1 %collective-permute-start = (bf16[8,8192]{1,0:T(8,128)(2,1)S(1)}, bf16[8,8192]{1,0:T(8,128)(2,1)S(1)}, u32[]{:S(2)}, u32[]{:S(2)}) collective-permute-start(bf16[8,8192]{1,0:T(8,128)(2,1)S(1)} %get-tuple-element.16), channel_id=1, source_target_pairs={{0,4},{1,5},{2,6},{3,7},{4,0},{5,1},{6,2},{7,3},{8,12},{9,13},{10,... | collective-permute-start | bytes 393224 | tf_op jit(solution)/shard_map/ppermute | solution.py:16
  6.1 1.3 collective-permute-start.1
  7.5 2.6 %collective-permute-start.2 = (bf16[8,8192]{1,0:T(8,128)(2,1)S(1)}, bf16[8,8192]{1,0:T(8,128)(2,1)S(1)}, u32[]{:S(2)}, u32[]{:S(2)}) collective-permute-start(bf16[8,8192]{1,0:T(8,128)(2,1)S(1)} %get-tuple-element.15), channel_id=1, source_target_pairs={{0,5},{1,4},{2,7},{3,6},{4,1},{5,0},{6,3},{7,2},{8,13},{9,12},{10,... | collective-permute-start | bytes 393224 | tf_op jit(solution)/shard_map/ppermute | solution.py:16
  11.0 15.1 %compare_select_fusion.refs_4_.refs_8_.refs_2_ = bf16[8192,1024]{1,0:T(8,128)(2,1)} fusion(bf16[8192,1024]{1,0:T(8,128)(2,1)} %param.5, s32[1024]{0:T(1024)} %param.7, s32[8192]{0:T(1024)} %param.6), kind=kLoop, calls=%fused_computation | loop fusion | flops 16777216 | bytes 33591296 | tf_op jit(solution)/shard_map/jit(_where)/select_n | solution.py:99
  26.1 2.5 %collective-permute-done.2.refs_2_ = bf16[8,8192]{1,0:T(8,128)(2,1)S(1)} collective-permute-done((bf16[8,8192]{1,0:T(8,128)(2,1)S(1)}, bf16[8,8192]{1,0:T(8,128)(2,1)S(1)}, u32[]{:S(2)}, u32[]{:S(2)}) %collective-permute-start.2) | collective-permute-done | bytes 131104 | tf_op jit(solution)/shard_map/ppermute | solution.py:16
  28.6 5.8 %copy-done = bf16[8192,1024]{1,0:T(8,128)(2,1)S(1)} copy-done((bf16[8192,1024]{1,0:T(8,128)(2,1)S(1)}, bf16[8192,1024]{1,0:T(8,128)(2,1)}, u32[]{:S(2)}) %copy-start) | copy-done | bytes 16777240
  36.8 0.9 shard_map.48
  37.7 1.5 collective-permute-start.6
  39.2 2.2 %constant_dynamic-slice_fusion.10 = (bf16[24,8192]{1,0:T(8,128)(2,1)S(1)}, bf16[24,8192]{1,0:T(8,128)(2,1)S(1)}, bf16[24,8192]{1,0:T(8,128)(2,1)S(1)}, bf16[24,8192]{1,0:T(8,128)(2,1)S(1)}) fusion(bf16[48,65536]{1,0:T(8,128)(2,1)} %param.4, s32[]{:T(128)S(6)} %select_n.39, s32[]{:T(128)S(6)} %select_n.36, s32[]{:T(128)S(6)} %select_n.37, s32[]{:T(128)S(6)} %select_n.38), kind=kLoop, calls=%fused_computation.23 | loop fusion | bytes 3145744 | tf_op jit(solution)/shard_map/dynamic_slice | solution.py:112
  41.4 4.4 %collective-permute-start.21 = (bf16[24,8192]{1,0:T(8,128)(2,1)S(1)}, bf16[24,8192]{1,0:T(8,128)(2,1)S(1)}, u32[]{:S(2)}, u32[]{:S(2)}) collective-permute-start(bf16[24,8192]{1,0:T(8,128)(2,1)S(1)} %get-tuple-element.14), channel_id=1, source_target_pairs={{0,4},{1,5},{2,6},{3,7},{4,0},{5,1},{6,2},{7,3},{8,12},{9,13},{10,... | collective-permute-start | bytes 1179656 | tf_op jit(solution)/shard_map/ppermute | solution.py:16
  47.3 2.1 constant_dynamic-slice_fusion.12
  50.5 2.8 %collective-permute-start.22 = (bf16[24,8192]{1,0:T(8,128)(2,1)S(1)}, bf16[24,8192]{1,0:T(8,128)(2,1)S(1)}, u32[]{:S(2)}, u32[]{:S(2)}) collective-permute-start(bf16[24,8192]{1,0:T(8,128)(2,1)S(1)} %get-tuple-element.11), channel_id=1, source_target_pairs={{0,5},{1,4},{2,7},{3,6},{4,1},{5,0},{6,3},{7,2},{8,13},{9,12},{10,... | collective-permute-start | bytes 1179656 | tf_op jit(solution)/shard_map/ppermute | solution.py:16
  53.2 2.9 %collective-permute-start.26 = (bf16[24,8192]{1,0:T(8,128)(2,1)S(1)}, bf16[24,8192]{1,0:T(8,128)(2,1)S(1)}, u32[]{:S(2)}, u32[]{:S(2)}) collective-permute-start(bf16[24,8192]{1,0:T(8,128)(2,1)S(1)} %get-tuple-element.13), channel_id=1, source_target_pairs={{0,6},{1,7},{2,4},{3,5},{4,2},{5,3},{6,0},{7,1},{8,14},{9,15},{10,... | collective-permute-start | bytes 1179656 | tf_op jit(solution)/shard_map/ppermute | solution.py:16
  56.2 34.8 %collective-permute-done.21.refs_0_ = bf16[24,8192]{1,0:T(8,128)(2,1)S(1)} collective-permute-done((bf16[24,8192]{1,0:T(8,128)(2,1)S(1)}, bf16[24,8192]{1,0:T(8,128)(2,1)S(1)}, u32[]{:S(2)}, u32[]{:S(2)}) %collective-permute-start.21) | collective-permute-done | bytes 393248 | tf_op jit(solution)/shard_map/ppermute | solution.py:16
  91.0 2.3 %collective-permute-start.27 = (bf16[24,8192]{1,0:T(8,128)(2,1)S(1)}, bf16[24,8192]{1,0:T(8,128)(2,1)S(1)}, u32[]{:S(2)}, u32[]{:S(2)}) collective-permute-start(bf16[24,8192]{1,0:T(8,128)(2,1)S(1)} %get-tuple-element.12), channel_id=1, source_target_pairs={{0,7},{1,6},{2,5},{3,4},{4,3},{5,2},{6,1},{7,0},{8,15},{9,14},{10,... | collective-permute-start | bytes 1179656 | tf_op jit(solution)/shard_map/ppermute | solution.py:16
  93.3 2.0 constant_dynamic-slice_fusion
  95.4 24.3 %collective-permute-done.22.refs_1_ = bf16[24,8192]{1,0:T(8,128)(2,1)S(1)} collective-permute-done((bf16[24,8192]{1,0:T(8,128)(2,1)S(1)}, bf16[24,8192]{1,0:T(8,128)(2,1)S(1)}, u32[]{:S(2)}, u32[]{:S(2)}) %collective-permute-start.22) | collective-permute-done | bytes 393248 | tf_op jit(solution)/shard_map/ppermute | solution.py:16
  119.6 0.9 collective-permute-start.13
  120.5 16.9 %collective-permute-start.14 = (bf16[48,8192]{1,0:T(8,128)(2,1)S(1)}, bf16[48,8192]{1,0:T(8,128)(2,1)S(1)}, u32[]{:S(2)}, u32[]{:S(2)}) collective-permute-start(bf16[48,8192]{1,0:T(8,128)(2,1)S(1)} %get-tuple-element.17), channel_id=1, source_target_pairs={{0,3},{1,2},{2,1},{3,0},{4,7},{5,6},{6,5},{7,4},{8,11},{9,10},{10,... | collective-permute-start | bytes 2359304 | tf_op jit(solution)/shard_map/ppermute | solution.py:16
  137.4 5.8 %copy-done.1 = bf16[8192,1024]{1,0:T(8,128)(2,1)S(1)} copy-done((bf16[8192,1024]{1,0:T(8,128)(2,1)S(1)}, bf16[8192,1024]{1,0:T(8,128)(2,1)}, u32[]{:S(2)}) %copy-start.1) | copy-done | bytes 16777240
  143.2 0.9 shard_map.57
  144.0 0.9 shard_map.61
  146.4 2.6 %collective-permute-start.11 = (bf16[16,8192]{1,0:T(8,128)(2,1)S(1)}, bf16[16,8192]{1,0:T(8,128)(2,1)S(1)}, u32[]{:S(2)}, u32[]{:S(2)}) collective-permute-start(bf16[16,8192]{1,0:T(8,128)(2,1)S(1)} %get-tuple-element.21), channel_id=1, source_target_pairs={{0,7},{1,6},{2,5},{3,4},{4,3},{5,2},{6,1},{7,0},{8,15},{9,14},{10,... | collective-permute-start | bytes 786440 | tf_op jit(solution)/shard_map/ppermute | solution.py:16
  149.0 0.9 shard_map.56
  149.9 0.9 shard_map.54
  150.8 0.9 shard_map.55
  151.7 0.9 shard_map.60
  152.6 0.9 shard_map.58
  153.5 0.9 shard_map.59
  154.4 14.8 %collective-permute-done.10.refs_2_ = bf16[16,8192]{1,0:T(8,128)(2,1)S(1)} collective-permute-done((bf16[16,8192]{1,0:T(8,128)(2,1)S(1)}, bf16[16,8192]{1,0:T(8,128)(2,1)S(1)}, u32[]{:S(2)}, u32[]{:S(2)}) %collective-permute-start.10) | collective-permute-done | bytes 262176 | tf_op jit(solution)/shard_map/ppermute | solution.py:16
  170.4 1.4 collective-permute-start.30
  171.8 1.3 shard_map.53
  173.2 1.3 collective-permute-done.30
  174.6 1.1 collective-permute-start.31
  175.7 1.5 shard_map.51
  177.3 1.3 shard_map.52
  178.6 1.4 collective-permute-start.17
  180.0 1.3 shard_map.50
  181.3 6.0 %collective-permute-done.17 = f32[256,256]{1,0:T(8,128)S(1)} collective-permute-done((f32[256,256]{1,0:T(8,128)S(1)}, f32[256,256]{1,0:T(8,128)S(1)}, u32[]{:S(2)}, u32[]{:S(2)}) %collective-permute-start.17) | collective-permute-done | bytes 262176 | tf_op jit(solution)/shard_map/ppermute | solution.py:16
  187.5 1.1 collective-permute-start.18
  188.6 11.3 %collective-permute-start.32 = (f32[24,256]{1,0:T(8,128)S(1)}, f32[24,256]{1,0:T(8,128)S(1)}, u32[]{:S(2)}, u32[]{:S(2)}) collective-permute-start(f32[24,256]{1,0:T(8,128)S(1)} %slice_add_fusion.1), channel_id=1, source_target_pairs={{0,2},{1,3},{2,0},{3,1},{4,6},{5,7},{6,4},{7,5},{8,10},{9,11},{10,... | collective-permute-start | bytes 73736 | tf_op jit(solution)/shard_map/ppermute | solution.py:16
  199.9 4.1 %collective-permute-start.19 = (f32[72,256]{1,0:T(8,128)S(1)}, f32[72,256]{1,0:T(8,128)S(1)}, u32[]{:S(2)}, u32[]{:S(2)}) collective-permute-start(f32[72,256]{1,0:T(8,128)S(1)} %pad_maximum_fusion.1), channel_id=1, source_target_pairs={{0,2},{1,3},{2,0},{3,1},{4,6},{5,7},{6,4},{7,5},{8,10},{9,11},{10,... | collective-permute-start | bytes 221192 | tf_op jit(solution)/shard_map/ppermute | solution.py:16
  204.1 3.2 %collective-permute-start.34 = (f32[24,256]{1,0:T(8,128)S(1)}, f32[24,256]{1,0:T(8,128)S(1)}, u32[]{:S(2)}, u32[]{:S(2)}) collective-permute-start(f32[24,256]{1,0:T(8,128)S(1)} %get-tuple-element.35), channel_id=1, source_target_pairs={{0,5},{1,4},{2,7},{3,6},{4,1},{5,0},{6,3},{7,2},{8,13},{9,12},{10,... | collective-permute-start | bytes 73736 | tf_op jit(solution)/shard_map/ppermute | solution.py:16
  207.4 1.0 collective-permute-start.20
  208.8 1.3 collective-permute-done.34
  210.1 2.1 collective-permute-done.20
  (91 shorter events, 9.9 us)
Async XLA Ops:
  2.0 24.1 %collective-permute-start = (bf16[8,8192]{1,0:T(8,128)(2,1)S(1)}, bf16[8,8192]{1,0:T(8,128)(2,1)S(1)}, u32[]{:S(2)}, u32[]{:S(2)}) collective-permute-start(bf16[8,8192]{1,0:T(8,128)(2,1)S(1)} %get-tuple-element.16), channel_id=1, source_target_pairs={{0,4},{1,5},{2,6},{3,7},{4,0},{5,1},{6,2},{7,3},{8,12},{9,13},{10,... | collective-permute-start | bytes 393224 | tf_op jit(solution)/shard_map/ppermute | solution.py:16
  6.1 20.0 %collective-permute-start.1 = (bf16[8,8192]{1,0:T(8,128)(2,1)S(1)}, bf16[8,8192]{1,0:T(8,128)(2,1)S(1)}, u32[]{:S(2)}, u32[]{:S(2)}) collective-permute-start(bf16[8,8192]{1,0:T(8,128)(2,1)S(1)} %get-tuple-element.9), channel_id=1, source_target_pairs={{0,6},{1,7},{2,4},{3,5},{4,2},{5,3},{6,0},{7,1},{8,14},{9,15},{10,... | collective-permute-start | bytes 393224 | tf_op jit(solution)/shard_map/ppermute | solution.py:16
  7.5 21.1 %collective-permute-start.2 = (bf16[8,8192]{1,0:T(8,128)(2,1)S(1)}, bf16[8,8192]{1,0:T(8,128)(2,1)S(1)}, u32[]{:S(2)}, u32[]{:S(2)}) collective-permute-start(bf16[8,8192]{1,0:T(8,128)(2,1)S(1)} %get-tuple-element.15), channel_id=1, source_target_pairs={{0,5},{1,4},{2,7},{3,6},{4,1},{5,0},{6,3},{7,2},{8,13},{9,12},{10,... | collective-permute-start | bytes 393224 | tf_op jit(solution)/shard_map/ppermute | solution.py:16
  10.1 18.5 %collective-permute-start.3 = (bf16[8,8192]{1,0:T(8,128)(2,1)S(1)}, bf16[8,8192]{1,0:T(8,128)(2,1)S(1)}, u32[]{:S(2)}, u32[]{:S(2)}) collective-permute-start(bf16[8,8192]{1,0:T(8,128)(2,1)S(1)} %get-tuple-element.10), channel_id=1, source_target_pairs={{0,7},{1,6},{2,5},{3,4},{4,3},{5,2},{6,1},{7,0},{8,15},{9,14},{10,... | collective-permute-start | bytes 393224 | tf_op jit(solution)/shard_map/ppermute | solution.py:16
  28.6 5.8 %copy-start = (bf16[8192,1024]{1,0:T(8,128)(2,1)S(1)}, bf16[8192,1024]{1,0:T(8,128)(2,1)}, u32[]{:S(2)}) copy-start(bf16[8192,1024]{1,0:T(8,128)(2,1)} %compare_select_fusion.refs_4_.refs_8_.refs_2_) | copy-start | bytes 50331652
  35.2 10.6 %slice-start = ((s8[16777216]{0:T(1024)(128)(4,1)}), s8[4194304]{0:T(1024)(128)(4,1)S(1)}, s32[]{:S(2)}) async-start(s8[16777216]{0:T(1024)(128)(4,1)} %bitcast.1), calls=%async_computation | async-start | bytes 8388608
  35.2 10.5 %slice-start.1 = ((s8[16777216]{0:T(1024)(128)(4,1)}), s8[4194304]{0:T(1024)(128)(4,1)S(1)}, s32[]{:S(2)}) async-start(s8[16777216]{0:T(1024)(128)(4,1)} %bitcast.1), calls=%async_computation.1 | async-start | bytes 8388608
  35.2 2.4 %collective-permute-start.5 = (f32[32,256]{1,0:T(8,128)S(1)}, f32[32,256]{1,0:T(8,128)S(1)}, u32[]{:S(2)}, u32[]{:S(2)}) collective-permute-start(f32[32,256]{1,0:T(8,128)S(1)} %shard_map.49), channel_id=1, source_target_pairs={{0,8},{8,0},{16,24},{24,16},{1,9},{9,1},{17,25},{25,17},{2,10},{10... | collective-permute-start | bytes 98312 | tf_op jit(solution)/shard_map/ppermute | solution.py:16
  36.2 9.6 %slice-start.2 = ((s8[16777216]{0:T(1024)(128)(4,1)}), s8[4194304]{0:T(1024)(128)(4,1)S(1)}, s32[]{:S(2)}) async-start(s8[16777216]{0:T(1024)(128)(4,1)} %bitcast.1), calls=%async_computation.2 | async-start | bytes 8388608
  36.2 9.6 %slice-start.3 = ((s8[16777216]{0:T(1024)(128)(4,1)}), s8[4194304]{0:T(1024)(128)(4,1)S(1)}, s32[]{:S(2)}) async-start(s8[16777216]{0:T(1024)(128)(4,1)} %bitcast.1), calls=%async_computation.3 | async-start | bytes 8388608
  36.2 10.5 %collective-permute-start.4 = (f32[32,256]{1,0:T(8,128)S(1)}, f32[32,256]{1,0:T(8,128)S(1)}, u32[]{:S(2)}, u32[]{:S(2)}) collective-permute-start(f32[32,256]{1,0:T(8,128)S(1)} %shard_map.47), channel_id=1, source_target_pairs={{0,8},{8,0},{16,24},{24,16},{1,9},{9,1},{17,25},{25,17},{2,10},{10... | collective-permute-start | bytes 98312 | tf_op jit(solution)/shard_map/ppermute | solution.py:16
  37.7 9.0 %collective-permute-start.6 = (f32[32,256]{1,0:T(8,128)S(1)}, f32[32,256]{1,0:T(8,128)S(1)}, u32[]{:S(2)}, u32[]{:S(2)}) collective-permute-start(f32[32,256]{1,0:T(8,128)S(1)} %add.94), channel_id=1, source_target_pairs={{0,16},{8,24},{16,0},{24,8},{1,17},{9,25},{17,1},{25,9},{2,18},{10... | collective-permute-start | bytes 98312 | tf_op jit(solution)/shard_map/ppermute | solution.py:16
  41.4 49.6 %collective-permute-start.21 = (bf16[24,8192]{1,0:T(8,128)(2,1)S(1)}, bf16[24,8192]{1,0:T(8,128)(2,1)S(1)}, u32[]{:S(2)}, u32[]{:S(2)}) collective-permute-start(bf16[24,8192]{1,0:T(8,128)(2,1)S(1)} %get-tuple-element.14), channel_id=1, source_target_pairs={{0,4},{1,5},{2,6},{3,7},{4,0},{5,1},{6,2},{7,3},{8,12},{9,13},{10,... | collective-permute-start | bytes 1179656 | tf_op jit(solution)/shard_map/ppermute | solution.py:16
  46.7 6.5 %collective-permute-start.7 = (f32[16,256]{1,0:T(8,128)S(1)}, f32[16,256]{1,0:T(8,128)S(1)}, u32[]{:S(2)}, u32[]{:S(2)}) collective-permute-start(f32[16,256]{1,0:T(8,128)S(1)} %slice.84), channel_id=1, source_target_pairs={{0,1},{1,0},{2,3},{3,2},{4,5},{5,4},{6,7},{7,6},{8,9},{9,8},{10,11... | collective-permute-start | bytes 49160 | tf_op jit(solution)/shard_map/ppermute | solution.py:16
  49.4 95.6 %collective-permute-start.8 = (bf16[16,8192]{1,0:T(8,128)(2,1)}, bf16[16,8192]{1,0:T(8,128)(2,1)S(1)}, u32[]{:S(2)}, u32[]{:S(2)}) collective-permute-start(bf16[16,8192]{1,0:T(8,128)(2,1)} %get-tuple-element.24), channel_id=1, source_target_pairs={{0,4},{1,5},{2,6},{3,7},{4,0},{5,1},{6,2},{7,3},{8,12},{9,13},{10,... | collective-permute-start | bytes 786440 | tf_op jit(solution)/shard_map/ppermute | solution.py:16
  49.6 95.4 %collective-permute-start.9 = (bf16[16,8192]{1,0:T(8,128)(2,1)}, bf16[16,8192]{1,0:T(8,128)(2,1)S(1)}, u32[]{:S(2)}, u32[]{:S(2)}) collective-permute-start(bf16[16,8192]{1,0:T(8,128)(2,1)} %get-tuple-element.23), channel_id=1, source_target_pairs={{0,6},{1,7},{2,4},{3,5},{4,2},{5,3},{6,0},{7,1},{8,14},{9,15},{10,... | collective-permute-start | bytes 786440 | tf_op jit(solution)/shard_map/ppermute | solution.py:16
  50.5 69.2 %collective-permute-start.22 = (bf16[24,8192]{1,0:T(8,128)(2,1)S(1)}, bf16[24,8192]{1,0:T(8,128)(2,1)S(1)}, u32[]{:S(2)}, u32[]{:S(2)}) collective-permute-start(bf16[24,8192]{1,0:T(8,128)(2,1)S(1)} %get-tuple-element.11), channel_id=1, source_target_pairs={{0,5},{1,4},{2,7},{3,6},{4,1},{5,0},{6,3},{7,2},{8,13},{9,12},{10,... | collective-permute-start | bytes 1179656 | tf_op jit(solution)/shard_map/ppermute | solution.py:16
  53.2 66.4 %collective-permute-start.26 = (bf16[24,8192]{1,0:T(8,128)(2,1)S(1)}, bf16[24,8192]{1,0:T(8,128)(2,1)S(1)}, u32[]{:S(2)}, u32[]{:S(2)}) collective-permute-start(bf16[24,8192]{1,0:T(8,128)(2,1)S(1)} %get-tuple-element.13), channel_id=1, source_target_pairs={{0,6},{1,7},{2,4},{3,5},{4,2},{5,3},{6,0},{7,1},{8,14},{9,15},{10,... | collective-permute-start | bytes 1179656 | tf_op jit(solution)/shard_map/ppermute | solution.py:16
  91.0 29.6 %collective-permute-start.27 = (bf16[24,8192]{1,0:T(8,128)(2,1)S(1)}, bf16[24,8192]{1,0:T(8,128)(2,1)S(1)}, u32[]{:S(2)}, u32[]{:S(2)}) collective-permute-start(bf16[24,8192]{1,0:T(8,128)(2,1)S(1)} %get-tuple-element.12), channel_id=1, source_target_pairs={{0,7},{1,6},{2,5},{3,4},{4,3},{5,2},{6,1},{7,0},{8,15},{9,14},{10,... | collective-permute-start | bytes 1179656 | tf_op jit(solution)/shard_map/ppermute | solution.py:16
  119.6 50.1 %collective-permute-start.12 = (bf16[48,8192]{1,0:T(8,128)(2,1)S(1)}, bf16[48,8192]{1,0:T(8,128)(2,1)S(1)}, u32[]{:S(2)}, u32[]{:S(2)}) collective-permute-start(bf16[48,8192]{1,0:T(8,128)(2,1)S(1)} %get-tuple-element.19), channel_id=1, source_target_pairs={{0,2},{1,3},{2,0},{3,1},{4,6},{5,7},{6,4},{7,5},{8,10},{9,11},{10,... | collective-permute-start | bytes 2359304 | tf_op jit(solution)/shard_map/ppermute | solution.py:16
  119.6 50.7 %collective-permute-start.13 = (bf16[48,8192]{1,0:T(8,128)(2,1)S(1)}, bf16[48,8192]{1,0:T(8,128)(2,1)S(1)}, u32[]{:S(2)}, u32[]{:S(2)}) collective-permute-start(bf16[48,8192]{1,0:T(8,128)(2,1)S(1)} %get-tuple-element.18), channel_id=1, source_target_pairs={{0,1},{1,0},{2,3},{3,2},{4,5},{5,4},{6,7},{7,6},{8,9},{9,8},{10,11... | collective-permute-start | bytes 2359304 | tf_op jit(solution)/shard_map/ppermute | solution.py:16
  120.5 51.3 %collective-permute-start.14 = (bf16[48,8192]{1,0:T(8,128)(2,1)S(1)}, bf16[48,8192]{1,0:T(8,128)(2,1)S(1)}, u32[]{:S(2)}, u32[]{:S(2)}) collective-permute-start(bf16[48,8192]{1,0:T(8,128)(2,1)S(1)} %get-tuple-element.17), channel_id=1, source_target_pairs={{0,3},{1,2},{2,1},{3,0},{4,7},{5,6},{6,5},{7,4},{8,11},{9,10},{10,... | collective-permute-start | bytes 2359304 | tf_op jit(solution)/shard_map/ppermute | solution.py:16
  137.4 5.8 %copy-start.1 = (bf16[8192,1024]{1,0:T(8,128)(2,1)S(1)}, bf16[8192,1024]{1,0:T(8,128)(2,1)}, u32[]{:S(2)}) copy-start(bf16[8192,1024]{1,0:T(8,128)(2,1)} %compare_select_fusion.refs_4_.refs_8_.refs_2_) | copy-start | bytes 50331652
  144.9 1.3 collective-permute-start.24
  145.0 1.4 collective-permute-start.29
  146.2 23.0 %collective-permute-start.10 = (bf16[16,8192]{1,0:T(8,128)(2,1)S(1)}, bf16[16,8192]{1,0:T(8,128)(2,1)S(1)}, u32[]{:S(2)}, u32[]{:S(2)}) collective-permute-start(bf16[16,8192]{1,0:T(8,128)(2,1)S(1)} %get-tuple-element.22), channel_id=1, source_target_pairs={{0,5},{1,4},{2,7},{3,6},{4,1},{5,0},{6,3},{7,2},{8,13},{9,12},{10,... | collective-permute-start | bytes 786440 | tf_op jit(solution)/shard_map/ppermute | solution.py:16
  146.4 22.9 %collective-permute-start.11 = (bf16[16,8192]{1,0:T(8,128)(2,1)S(1)}, bf16[16,8192]{1,0:T(8,128)(2,1)S(1)}, u32[]{:S(2)}, u32[]{:S(2)}) collective-permute-start(bf16[16,8192]{1,0:T(8,128)(2,1)S(1)} %get-tuple-element.21), channel_id=1, source_target_pairs={{0,7},{1,6},{2,5},{3,4},{4,3},{5,2},{6,1},{7,0},{8,15},{9,14},{10,... | collective-permute-start | bytes 786440 | tf_op jit(solution)/shard_map/ppermute | solution.py:16
  152.6 19.3 %slice-start.4 = ((s8[16777216]{0:T(1024)(128)(4,1)}), s8[4194304]{0:T(1024)(128)(4,1)S(1)}, s32[]{:S(2)}) async-start(s8[16777216]{0:T(1024)(128)(4,1)} %bitcast.3), calls=%async_computation.4 | async-start | bytes 8388608
  152.6 19.2 %slice-start.5 = ((s8[16777216]{0:T(1024)(128)(4,1)}), s8[4194304]{0:T(1024)(128)(4,1)S(1)}, s32[]{:S(2)}) async-start(s8[16777216]{0:T(1024)(128)(4,1)} %bitcast.3), calls=%async_computation.5 | async-start | bytes 8388608
  153.5 18.4 %slice-start.6 = ((s8[16777216]{0:T(1024)(128)(4,1)}), s8[4194304]{0:T(1024)(128)(4,1)S(1)}, s32[]{:S(2)}) async-start(s8[16777216]{0:T(1024)(128)(4,1)} %bitcast.3), calls=%async_computation.6 | async-start | bytes 8388608
  153.5 18.4 %slice-start.7 = ((s8[16777216]{0:T(1024)(128)(4,1)}), s8[4194304]{0:T(1024)(128)(4,1)S(1)}, s32[]{:S(2)}) async-start(s8[16777216]{0:T(1024)(128)(4,1)} %bitcast.3), calls=%async_computation.7 | async-start | bytes 8388608
  169.3 10.7 %collective-permute-start.23 = (f32[48,256]{1,0:T(8,128)S(1)}, f32[48,256]{1,0:T(8,128)S(1)}, u32[]{:S(2)}, u32[]{:S(2)}) collective-permute-start(f32[48,256]{1,0:T(8,128)S(1)} %shard_map.55), channel_id=1, source_target_pairs={{0,8},{8,0},{16,24},{24,16},{1,9},{9,1},{17,25},{25,17},{2,10},{10... | collective-permute-start | bytes 147464 | tf_op jit(solution)/shard_map/ppermute | solution.py:16
  169.3 4.0 %collective-permute-start.28 = (f32[48,256]{1,0:T(8,128)S(1)}, f32[48,256]{1,0:T(8,128)S(1)}, u32[]{:S(2)}, u32[]{:S(2)}) collective-permute-start(f32[48,256]{1,0:T(8,128)S(1)} %shard_map.59), channel_id=1, source_target_pairs={{0,8},{8,0},{16,24},{24,16},{1,9},{9,1},{17,25},{25,17},{2,10},{10... | collective-permute-start | bytes 147464 | tf_op jit(solution)/shard_map/ppermute | solution.py:16
  169.8 10.2 %collective-permute-start.25 = (f32[48,256]{1,0:T(8,128)S(1)}, f32[48,256]{1,0:T(8,128)S(1)}, u32[]{:S(2)}, u32[]{:S(2)}) collective-permute-start(f32[48,256]{1,0:T(8,128)S(1)} %add.107), channel_id=1, source_target_pairs={{0,16},{8,24},{16,0},{24,8},{1,17},{9,25},{17,1},{25,9},{2,18},{10... | collective-permute-start | bytes 147464 | tf_op jit(solution)/shard_map/ppermute | solution.py:16
  170.4 4.2 %collective-permute-start.30 = (f32[48,256]{1,0:T(8,128)S(1)}, f32[48,256]{1,0:T(8,128)S(1)}, u32[]{:S(2)}, u32[]{:S(2)}) collective-permute-start(f32[48,256]{1,0:T(8,128)S(1)} %add.110), channel_id=1, source_target_pairs={{0,16},{8,24},{16,0},{24,8},{1,17},{9,25},{17,1},{25,9},{2,18},{10... | collective-permute-start | bytes 147464 | tf_op jit(solution)/shard_map/ppermute | solution.py:16
  173.1 5.4 %collective-permute-start.16 = (f32[256,256]{1,0:T(8,128)S(1)}, f32[256,256]{1,0:T(8,128)S(1)}, u32[]{:S(2)}, u32[]{:S(2)}) collective-permute-start(f32[256,256]{1,0:T(8,128)S(1)} %shard_map.53), channel_id=1, source_target_pairs={{0,8},{8,0},{16,24},{24,16},{1,9},{9,1},{17,25},{25,17},{2,10},{10... | collective-permute-start | bytes 786440 | tf_op jit(solution)/shard_map/ppermute | solution.py:16
  174.6 14.0 %collective-permute-start.31 = (f32[24,256]{1,0:T(8,128)S(1)}, f32[24,256]{1,0:T(8,128)S(1)}, u32[]{:S(2)}, u32[]{:S(2)}) collective-permute-start(f32[24,256]{1,0:T(8,128)S(1)} %slice.98), channel_id=1, source_target_pairs={{0,1},{1,0},{2,3},{3,2},{4,5},{5,4},{6,7},{7,6},{8,9},{9,8},{10,11... | collective-permute-start | bytes 73736 | tf_op jit(solution)/shard_map/ppermute | solution.py:16
  177.2 4.2 %collective-permute-start.15 = (f32[256,256]{1,0:T(8,128)S(1)}, f32[256,256]{1,0:T(8,128)S(1)}, u32[]{:S(2)}, u32[]{:S(2)}) collective-permute-start(f32[256,256]{1,0:T(8,128)S(1)} %shard_map.51), channel_id=1, source_target_pairs={{0,8},{8,0},{16,24},{24,16},{1,9},{9,1},{17,25},{25,17},{2,10},{10... | collective-permute-start | bytes 786440 | tf_op jit(solution)/shard_map/ppermute | solution.py:16
  178.6 8.7 %collective-permute-start.17 = (f32[256,256]{1,0:T(8,128)S(1)}, f32[256,256]{1,0:T(8,128)S(1)}, u32[]{:S(2)}, u32[]{:S(2)}) collective-permute-start(f32[256,256]{1,0:T(8,128)S(1)} %add.102), channel_id=1, source_target_pairs={{0,16},{8,24},{16,0},{24,8},{1,17},{9,25},{17,1},{25,9},{2,18},{10... | collective-permute-start | bytes 786440 | tf_op jit(solution)/shard_map/ppermute | solution.py:16
  187.5 12.4 %collective-permute-start.18 = (f32[128,256]{1,0:T(8,128)S(1)}, f32[128,256]{1,0:T(8,128)S(1)}, u32[]{:S(2)}, u32[]{:S(2)}) collective-permute-start(f32[128,256]{1,0:T(8,128)S(1)} %pad_maximum_fusion), channel_id=1, source_target_pairs={{0,1},{1,0},{2,3},{3,2},{4,5},{5,4},{6,7},{7,6},{8,9},{9,8},{10,11... | collective-permute-start | bytes 393224 | tf_op jit(solution)/shard_map/ppermute | solution.py:16
  188.6 15.5 %collective-permute-start.32 = (f32[24,256]{1,0:T(8,128)S(1)}, f32[24,256]{1,0:T(8,128)S(1)}, u32[]{:S(2)}, u32[]{:S(2)}) collective-permute-start(f32[24,256]{1,0:T(8,128)S(1)} %slice_add_fusion.1), channel_id=1, source_target_pairs={{0,2},{1,3},{2,0},{3,1},{4,6},{5,7},{6,4},{7,5},{8,10},{9,11},{10,... | collective-permute-start | bytes 73736 | tf_op jit(solution)/shard_map/ppermute | solution.py:16
  199.9 7.4 %collective-permute-start.19 = (f32[72,256]{1,0:T(8,128)S(1)}, f32[72,256]{1,0:T(8,128)S(1)}, u32[]{:S(2)}, u32[]{:S(2)}) collective-permute-start(f32[72,256]{1,0:T(8,128)S(1)} %pad_maximum_fusion.1), channel_id=1, source_target_pairs={{0,2},{1,3},{2,0},{3,1},{4,6},{5,7},{6,4},{7,5},{8,10},{9,11},{10,... | collective-permute-start | bytes 221192 | tf_op jit(solution)/shard_map/ppermute | solution.py:16
  204.0 4.8 %collective-permute-start.33 = (f32[24,256]{1,0:T(8,128)S(1)}, f32[24,256]{1,0:T(8,128)S(1)}, u32[]{:S(2)}, u32[]{:S(2)}) collective-permute-start(f32[24,256]{1,0:T(8,128)S(1)} %get-tuple-element.36), channel_id=1, source_target_pairs={{0,4},{1,5},{2,6},{3,7},{4,0},{5,1},{6,2},{7,3},{8,12},{9,13},{10,... | collective-permute-start | bytes 73736 | tf_op jit(solution)/shard_map/ppermute | solution.py:16
  204.1 6.0 %collective-permute-start.34 = (f32[24,256]{1,0:T(8,128)S(1)}, f32[24,256]{1,0:T(8,128)S(1)}, u32[]{:S(2)}, u32[]{:S(2)}) collective-permute-start(f32[24,256]{1,0:T(8,128)S(1)} %get-tuple-element.35), channel_id=1, source_target_pairs={{0,5},{1,4},{2,7},{3,6},{4,1},{5,0},{6,3},{7,2},{8,13},{9,12},{10,... | collective-permute-start | bytes 73736 | tf_op jit(solution)/shard_map/ppermute | solution.py:16
  207.4 4.8 %collective-permute-start.20 = (f32[24,256]{1,0:T(8,128)S(1)}, f32[24,256]{1,0:T(8,128)S(1)}, u32[]{:S(2)}, u32[]{:S(2)}) collective-permute-start(f32[24,256]{1,0:T(8,128)S(1)} %concatenate.24), channel_id=1, source_target_pairs={{0,4},{1,5},{2,6},{3,7},{4,0},{5,1},{6,2},{7,3},{8,12},{9,13},{10,... | collective-permute-start | bytes 73736 | tf_op jit(solution)/shard_map/ppermute | solution.py:16
